TPU v7x, 256 devices: a whole 4x4x8 slice. The times are simulated.
256 devices in a mesh: cube: 16 (over z, x_hi), row: 4 (over x_lo, core), col: 4 (over y).
Axes of the slice: x: 4 (x_hi: 2, x_lo: 2; x = x_hi * 2 + x_lo), y: 4, z: 8, core: 2. Of those that a mesh axis runs over, the one named last changes fastest.
Arguments:
- diag_block: float32 [16, 512, 512], P('cube'), as said below
- panel: float32 [16, 8192, 512], P('cube', ('row', 'col')), may hold values from -2.4 to 2.4
- trailing: float32 [16, 2048, 8192], P('cube', 'col', 'row'), may hold values from -6 to 6
- parent_front: float32 [16, 512, 8192], P('cube', 'col', 'row'), may hold values from -6 to 6
- front_order: int32 [16], P('cube'), may hold values from 4096 to 8192, as said below
- dest_group: int32 [16, 4, 4, 64, 1], P(None, 'col', 'row'), may hold values from 0 to 15; in each aligned block of 64 rows (0 to 63, 64 to 127, ..., all dimensions but the last counted through in order) at most 8 rows name the same one
- parent_block: int32 [16, 4, 4, 64, 1], P(None, 'col', 'row'), may hold values from 0 to 15
Outputs:
- assembled: float32 [16, 512, 8192], P('cube', 'col', 'row')
Inputs may be any that keep to these rules, and one draw needn't show every extreme that they name: `front_order`: a multiple of 128; each group's update matrix is zero in the columns at or beyond it. `dest_group`: at most 8 of the 64 blocks of one device and group go to one group. `diag_block`: symmetric positive definite.
All inputs are finite; a program needn't handle non-finite values.
Results may differ from a plain program's by a relative error of at most 0.0003.
Values sent between devices are 32-bit elements; how exact they have to be, the bound alone decides.
A program may use at most 128 MiB of HBM per device.

v0:
```python
import functools

import jax
import jax.numpy as jnp
from jax import lax
from jax.experimental import pallas as pl
from jax.experimental.pallas import tpu as pltpu
from jax.sharding import PartitionSpec as P

BS = 128


def spread(value, axis, root):
    mine = lax.axis_index(axis) == root
    return lax.psum(jnp.where(mine, value, jnp.zeros_like(value)), axis)


def shards(diag_block, panel, trailing, parent_front, front_order, dest_group, parent_block):
    precise_mode = lax.Precision.HIGHEST
    slab_rows = spread(panel[0], "row", 0)
    col_rows = lax.all_gather(panel[0], "col", axis=0, tiled=True)
    chol_inv = factor_inverse(diag_block[0])
    contract_t = (((1,), (1,)), ((), ()))
    slab_factor = lax.dot_general(slab_rows, chol_inv, contract_t, precision=precise_mode)
    col_factor = lax.dot_general(col_rows, chol_inv, contract_t, precision=precise_mode)
    product = lax.dot_general(slab_factor, col_factor, contract_t, precision=precise_mode)
    device_rows = trailing.shape[1]
    cols_dev = trailing.shape[2]
    column_ids = lax.axis_index("row") * cols_dev + jnp.arange(cols_dev, dtype=jnp.int32)
    update = jnp.where(
        column_ids[None, :] < front_order[0], trailing[0] - product, jnp.float32(0.0)
    )
    block_rows = device_rows // BS
    block_cols = cols_dev // BS
    nblocks = block_rows * block_cols
    groups = lax.axis_size("cube")
    own_group = lax.axis_index("cube")
    dest_all = dest_group[:, 0, 0, :, 0]
    parent_all = parent_block[:, 0, 0, :, 0]
    dest_mine = lax.dynamic_index_in_dim(dest_all, own_group, 0, keepdims=False)
    capacity = 2 * nblocks // groups
    nslots = groups * capacity
    hit_table = (dest_mine[:, None] == jnp.arange(groups, dtype=jnp.int32)[None, :]).astype(
        jnp.int32
    )
    before = jnp.cumsum(hit_table, axis=0) - hit_table
    slot_ids = jnp.sum(before * hit_table, axis=1)
    position = dest_mine * capacity + slot_ids
    source_of_slot = (
        jnp.full((nslots,), -1, jnp.int32)
        .at[position]
        .set(jnp.arange(nblocks, dtype=jnp.int32), mode="drop")
    )
    outgoing = pack_blocks(source_of_slot, update, block_cols)
    incoming = lax.all_to_all(
        outgoing.reshape(groups, capacity * BS, BS), "cube", split_axis=0, concat_axis=0, tiled=True
    )
    arriving = dest_all == own_group
    arriving_i = arriving.astype(jnp.int32)
    rank_ids = jnp.cumsum(arriving_i, axis=1) - arriving_i
    in_position = jnp.where(
        arriving,
        jnp.arange(groups, dtype=jnp.int32)[:, None] * capacity + rank_ids,
        nslots,
    )
    parent_of_slot = (
        jnp.full((nslots,), -1, jnp.int32)
        .at[in_position.reshape(-1)]
        .set(parent_all.reshape(-1), mode="drop")
    )
    assembled = combine_blocks(parent_of_slot, incoming.reshape(nslots, BS, BS), parent_front[0])
    return assembled[None]


def pack_kernel(block_cols, source_ref, update_ref, out_ref):
    def body(slot, carry):
        block = source_ref[slot]
        live = block >= 0
        block = jnp.maximum(block, 0)
        rows = pl.ds(pl.multiple_of((block // block_cols) * BS, BS), BS)
        cols = pl.ds(pl.multiple_of((block % block_cols) * BS, BS), BS)
        out_ref[slot] = jnp.where(live, update_ref[rows, cols], jnp.float32(0.0))
        return carry

    lax.fori_loop(0, out_ref.shape[0], body, 0)


def pack_blocks(source_of_slot, update, block_cols):
    nslots = source_of_slot.shape[0]
    return pl.pallas_call(
        functools.partial(pack_kernel, block_cols),
        out_shape=jax.ShapeDtypeStruct((nslots, BS, BS), update.dtype),
        in_specs=[
            pl.BlockSpec(memory_space=pltpu.SMEM),
            pl.BlockSpec(memory_space=pltpu.VMEM),
        ],
        out_specs=pl.BlockSpec(memory_space=pltpu.VMEM),
    )(source_of_slot, update)


def combine_kernel(parent_ref, incoming_ref, front_ref, out_ref):
    out_ref[...] = front_ref[...]

    def body(slot, carry):
        parent = parent_ref[slot]

        @pl.when(parent >= 0)
        def _():
            cols = pl.ds(pl.multiple_of(parent * BS, BS), BS)
            out_ref[:, cols] = out_ref[:, cols] + incoming_ref[slot]

        return carry

    lax.fori_loop(0, incoming_ref.shape[0], body, 0)


def combine_blocks(parent_of_slot, incoming, front):
    return pl.pallas_call(
        combine_kernel,
        out_shape=jax.ShapeDtypeStruct(front.shape, front.dtype),
        in_specs=[
            pl.BlockSpec(memory_space=pltpu.SMEM),
            pl.BlockSpec(memory_space=pltpu.VMEM),
            pl.BlockSpec(memory_space=pltpu.VMEM),
        ],
        out_specs=pl.BlockSpec(memory_space=pltpu.VMEM),
    )(parent_of_slot, incoming, front)


def factor_kernel(a_ref, inv_ref, work_ref, g_ref):
    n = a_ref.shape[0]
    nb = n // BS
    hp = lax.Precision.HIGHEST
    nt = (((1,), (1,)), ((), ()))
    work_ref[...] = a_ref[...]
    lane = lax.broadcasted_iota(jnp.int32, (1, 2 * BS), 1)
    sub = lax.broadcasted_iota(jnp.int32, (BS, BS), 0)
    col = lax.broadcasted_iota(jnp.int32, (BS, BS), 1)
    eye = (sub == col).astype(jnp.float32)
    diag_inv = []
    for k in range(nb):
        kk = pl.ds(k * BS, BS)
        g_ref[:, :BS] = work_ref[kk, kk]
        g_ref[:, BS:] = eye

        def step(j, carry):
            row = g_ref[pl.ds(j, 1), :]
            pivot = jnp.sum(jnp.where(lane == j, row, 0.0), axis=1, keepdims=True)
            scaled = row / jnp.sqrt(pivot)
            down = jnp.where(lane[:, :BS] > j, scaled[:, :BS], 0.0)
            down_col = jnp.transpose(jnp.broadcast_to(down, (BS, BS)))
            g = g_ref[...]
            g_ref[:, :BS] = g[:, :BS] - down_col * scaled[:, :BS]
            g_ref[:, BS:] = g[:, BS:] - down_col * scaled[:, BS:]
            g_ref[pl.ds(j, 1), :] = scaled
            return carry

        lax.fori_loop(0, BS, step, 0)
        upper = jnp.where(col >= sub, g_ref[:, :BS], 0.0)
        lk_inv = g_ref[:, BS:]
        diag_inv.append(lk_inv)
        work_ref[kk, kk] = jnp.transpose(upper)
        if k < nb - 1:
            rest = pl.ds((k + 1) * BS, n - (k + 1) * BS)
            panel = lax.dot_general(work_ref[rest, kk], lk_inv, nt, precision=hp,
                                    preferred_element_type=jnp.float32)
            work_ref[rest, kk] = panel
            work_ref[rest, rest] = work_ref[rest, rest] - lax.dot_general(
                panel, panel, nt, precision=hp, preferred_element_type=jnp.float32)
    inv_ref[...] = jnp.zeros_like(inv_ref)
    inv_ref[pl.ds(0, BS), pl.ds(0, BS)] = diag_inv[0]
    for i in range(1, nb):
        ii = pl.ds(i * BS, BS)
        left = pl.ds(0, i * BS)
        mixed = jnp.dot(work_ref[ii, left], inv_ref[left, left], precision=hp,
                        preferred_element_type=jnp.float32)
        inv_ref[ii, left] = -jnp.dot(diag_inv[i], mixed, precision=hp,
                                     preferred_element_type=jnp.float32)
        inv_ref[ii, ii] = diag_inv[i]


def factor_inverse(a):
    n = a.shape[0]
    return pl.pallas_call(
        factor_kernel,
        out_shape=jax.ShapeDtypeStruct((n, n), a.dtype),
        in_specs=[pl.BlockSpec(memory_space=pltpu.VMEM)],
        out_specs=pl.BlockSpec(memory_space=pltpu.VMEM),
        scratch_shapes=[pltpu.VMEM((n, n), jnp.float32), pltpu.VMEM((BS, 2 * BS), jnp.float32)],
    )(a)

def solution(mesh):
    placed = (
        P("cube", None, None),
        P("cube", ("row", "col"), None),
        P("cube", "col", "row"),
        P("cube", "col", "row"),
        P("cube"),
        P(None, "col", "row", None, None),
        P(None, "col", "row", None, None),
    )
    return jax.shard_map(
        shards, mesh=mesh, in_specs=placed, out_specs=P("cube", "col", "row"), check_vma=False
    )
```

profile of v0, /device:TPU:87, one launch (start us, length us, event | category | flops | bytes accessed | tf_op | source)
XLA Modules:
  0.0 368.7 jit_solution(15602250891235359351)
XLA Ops:
  7.4 0.0 all-reduce.2.cloned.1.call-start
  7.4 1.1 select_bitcast_fusion
  8.4 0.0 all-reduce.2.cloned.1.call-update
  8.5 0.0 all-gather.3.cloned.1.call-start
  8.5 0.5 all-gather.3.cloned.1.call-update
  9.7 0.0 copy-done.1
  9.7 0.1 fusion.3
  9.8 0.1 reduce_window_sum.26
  9.9 109.4 %shard_map.73 = f32[512,512]{1,0:T(8,128)} custom-call(f32[512,512]{1,0:T(8,128)} %bitcast.37), custom_call_target="tpu_custom_call" | custom-call | tf_op jit(solution)/shard_map/pallas_call | solution.py:184
  119.3 0.2 select_reduce_fusion
  119.5 1.3 scatter_custom_fusion.1.source_ref
  120.8 0.0 all-reduce.2.cloned.1.call-done
  120.8 3.4 fusion.10
  124.2 0.0 all-gather.3.cloned.1.call-done
  124.3 0.0 copy-start
  124.3 9.0 %fusion = f32[2048,512]{1,0:T(8,128)S(1)} fusion(f32[512,512]{1,0:T(8,128)} %shard_map.73, f32[1,2048,512]{2,1,0:T(8,128)} %all-gather.3.cloned.1.call-done), kind=kOutput, calls=%fused_computation.2 | convolution fusion | flops 6442450944 | bytes 9437184 | tf_op jit(solution)/shard_map/dot_general | solution.py:25
  133.3 0.0 copy-done
  133.3 8.5 %fusion.2.update_ref = f32[512,2048]{1,0:T(8,128)} fusion(f32[1,512,2048]{2,1,0:T(8,128)S(1)} %copy-done, f32[512,512]{1,0:T(8,128)S(1)} %fusion.10, f32[2048,512]{1,0:T(8,128)S(1)} %fusion, pred[2048]{0:T(1024)(128)(4,1)S(1)} %add_compare_fusion), kind=kOutput, calls=%fused_computation.5 | convolution fusion | flops 6444548096 | bytes 13633536 | tf_op jit(solution)/shard_map/dot_general | solution.py:26
  141.8 8.0 %shard_map.74 = f32[128,128,128]{2,1,0:T(8,128)} custom-call(s32[128]{0:T(128)} %scatter_custom_fusion.1.source_ref, f32[512,2048]{1,0:T(8,128)} %fusion.2.update_ref), custom_call_target="tpu_custom_call" | custom-call | tf_op jit(solution)/shard_map/pallas_call | solution.py:90
  149.9 10.1 %all-to-all-start = ((f32[16,1024,128]{2,1,0:T(8,128)}), f32[16,1024,128]{2,1,0:T(8,128)}, u32[]{:S(2)}, u32[]{:S(2)}) async-start(f32[16,1024,128]{2,1,0:T(8,128)} %bitcast.36), calls=%async_computation | async-start | bytes 16777216 | tf_op jit(solution)/shard_map/all_to_all | solution.py:55
  160.0 0.1 add.68
  160.1 0.1 add.69
  160.1 0.5 broadcast.100
  160.6 0.0 copy-done.2
  160.7 0.7 reduce.5
  161.3 0.1 reshape.111
  161.4 0.2 reduce_window_sum.24
  161.7 0.1 reduce_window_sum.25
  161.7 0.1 eq.38
  161.8 4.8 %scatter_custom_fusion.parent_ref = s32[128]{0:T(128)} fusion(s32[1024]{0:T(1024)S(1)} %bitcast.40, s32[1024]{0:T(1024)S(1)} %reshape.111, s32[]{:T(128)} %constant.12.clone.1), kind=kCustom, calls=%fused_computation.21 | custom fusion | bytes 516 | tf_op jit(solution)/shard_map/scatter | solution.py:69
  166.6 187.6 %all-to-all-done = f32[16,1024,128]{2,1,0:T(8,128)} async-done(((f32[16,1024,128]{2,1,0:T(8,128)}), f32[16,1024,128]{2,1,0:T(8,128)}, u32[]{:S(2)}, u32[]{:S(2)}) %all-to-all-start) | async-done | bytes 8388640 | tf_op jit(solution)/shard_map/all_to_all | solution.py:55
  354.3 7.0 %shard_map.75 = f32[128,2048]{1,0:T(8,128)} custom-call(s32[128]{0:T(128)} %scatter_custom_fusion.parent_ref, f32[128,128,128]{2,1,0:T(8,128)} %bitcast.12.incoming_ref, f32[128,2048]{1,0:T(8,128)} %bitcast.38), custom_call_target="tpu_custom_call" | custom-call | tf_op jit(solution)/shard_map/pallas_call | solution.py:118
  (9 shorter events, 0.1 us)
Async XLA Ops:
  7.4 2.3 copy-start.1
  7.4 113.5 %all-reduce.2.cloned.1.call-start = ((), (), s32[]{:S(2)}) async-start(), calls=%async_computation.1 | async-start | bytes 2097152 | tf_op jit(solution)/shard_map/psum | solution.py:15
  8.5 115.8 %all-gather.3.cloned.1.call-start = ((), (), s32[]{:S(2)}) async-start(), calls=%async_computation.2 | async-start | bytes 5242880 | tf_op jit(solution)/shard_map/all_gather | solution.py:21
  124.3 9.0 %copy-start = (f32[1,512,2048]{2,1,0:T(8,128)S(1)}, f32[1,512,2048]{2,1,0:T(8,128)}, u32[]{:S(2)}) copy-start(f32[1,512,2048]{2,1,0:T(8,128)} %param.9) | copy-start | bytes 12582916
  149.9 10.8 %copy-start.2 = (s32[16,1,1,64,1]{3,4,2,1,0:T(1,128)S(1)}, s32[16,1,1,64,1]{3,4,2,1,0:T(1,128)}, u32[]{:S(2)}) copy-start(s32[16,1,1,64,1]{3,4,2,1,0:T(1,128)} %param.13) | copy-start | bytes 12292
  149.9 204.4 %all-to-all-start = ((f32[16,1024,128]{2,1,0:T(8,128)}), f32[16,1024,128]{2,1,0:T(8,128)}, u32[]{:S(2)}, u32[]{:S(2)}) async-start(f32[16,1024,128]{2,1,0:T(8,128)} %bitcast.36), calls=%async_computation | async-start | bytes 16777216 | tf_op jit(solution)/shard_map/all_to_all | solution.py:55
Sparse Core Ops, SparseCore 0:
  10.9 49.1 all-reduce.1
Sparse Core Ops, SparseCore 1:
  10.9 53.0 all-gather.2
where the time goes:
time: 369 us
  waiting for transfers between devices  188 us (51%)
  Pallas kernels  124 us (34%)
  matrix products  20.9 us (6%)
  between operations  15.6 us (4%)
  starting transfers between devices  10.2 us (3%)
  local copies, waits for them, and re-layouts  7.01 us (2%)
    all_to_all x1, waiting for transfers between devices, shards(): lax.all_to_all(outgoing.reshape(groups, capacity * BS, BS), 'cube', split...  188 us
    pallas_call x1, Pallas kernels, factor_inverse(): pl.pallas_call(factor_kernel, out_shape=jax.ShapeDtypeStruct((n, n), a.dt...  109 us
    all_to_all x1, starting transfers between devices, shards(): lax.all_to_all(outgoing.reshape(groups, capacity * BS, BS), 'cube', split...  10.1 us
    dot_general x1, matrix products, shards(): lax.dot_general(col_rows, chol_inv, contract_t, precision=precise_mode)  8.97 us
    dot_general x1, matrix products, shards(): lax.dot_general(slab_factor, col_factor, contract_t, precision=precise_mode)  8.55 us
    pallas_call x1, Pallas kernels, pack_blocks(): pl.pallas_call(functools.partial(pack_kernel, block_cols), out_shape=jax....  8.04 us
  transfers between devices with their start and end apart: 3, of which 1 were waited for; matrix products, arithmetic and copies ran while one was open for 3% of the time, Pallas kernels for 30%

commit v1 on v0

--- a/solution.py
+++ b/solution.py
@@ -143,19 +143,25 @@
         g_ref[:, :BS] = work_ref[kk, kk]
         g_ref[:, BS:] = eye
 
-        def step(j, carry):
-            row = g_ref[pl.ds(j, 1), :]
-            pivot = jnp.sum(jnp.where(lane == j, row, 0.0), axis=1, keepdims=True)
-            scaled = row / jnp.sqrt(pivot)
-            down = jnp.where(lane[:, :BS] > j, scaled[:, :BS], 0.0)
-            down_col = jnp.transpose(jnp.broadcast_to(down, (BS, BS)))
-            g = g_ref[...]
-            g_ref[:, :BS] = g[:, :BS] - down_col * scaled[:, :BS]
-            g_ref[:, BS:] = g[:, BS:] - down_col * scaled[:, BS:]
-            g_ref[pl.ds(j, 1), :] = scaled
-            return carry
-
-        lax.fori_loop(0, BS, step, 0)
+        for lo in range(0, BS, 8):
+            height = BS - lo
+            rid = lo + lax.broadcasted_iota(jnp.int32, (height, 1), 0)
+
+            def step(j, carry, lo=lo, rid=rid):
+                row = g_ref[pl.ds(j, 1), :]
+                pivot = jnp.sum(jnp.where(lane == j, row, 0.0), axis=1, keepdims=True)
+                inv_d = 1.0 / jnp.sqrt(pivot)
+                scaled = row * inv_d
+                live = g_ref[lo:, :]
+                column = jnp.sum(
+                    jnp.where(lane[:, :BS] == j, live[:, :BS], 0.0), axis=1, keepdims=True
+                )
+                down = jnp.where(rid > j, column * inv_d, 0.0)
+                g_ref[lo:, :] = live - down * scaled
+                g_ref[pl.ds(j, 1), :] = scaled
+                return carry
+
+            lax.fori_loop(lo, lo + 8, step, 0, unroll=2)
         upper = jnp.where(col >= sub, g_ref[:, :BS], 0.0)
         lk_inv = g_ref[:, BS:]
         diag_inv.append(lk_inv)

time: 369 us -> 321 us (0.87)
  Pallas kernels: 124 us -> 76.9 us
    pallas_call x1, Pallas kernels: 109 us -> 61.9 us  [factor_inverse(): pl.pallas_call(factor_kernel, out_shape=jax.ShapeDtypeStruct((n, n), a.dt...]
  transfers between devices with their start and end apart: 3 -> 3, of which waited for: 1 -> 1; matrix products, arithmetic and copies ran while one was open for 3% -> 4% of each run, Pallas kernels for 30% -> 19%
where the time goes in v1:
time: 321 us
  waiting for transfers between devices  188 us (59%)
  Pallas kernels  76.9 us (24%)
  matrix products  20.9 us (7%)
  between operations  15.6 us (5%)
  starting transfers between devices  10.2 us (3%)
  local copies, waits for them, and re-layouts  7.01 us (2%)
    all_to_all x1, waiting for transfers between devices, shards(): lax.all_to_all(outgoing.reshape(groups, capacity * BS, BS), 'cube', split...  188 us
    pallas_call x1, Pallas kernels, factor_inverse(): pl.pallas_call(factor_kernel, out_shape=jax.ShapeDtypeStruct((n, n), a.dt...  61.9 us
    all_to_all x1, starting transfers between devices, shards(): lax.all_to_all(outgoing.reshape(groups, capacity * BS, BS), 'cube', split...  10.1 us
    dot_general x1, matrix products, shards(): lax.dot_general(col_rows, chol_inv, contract_t, precision=precise_mode)  8.96 us
    dot_general x1, matrix products, shards(): lax.dot_general(slab_factor, col_factor, contract_t, precision=precise_mode)  8.55 us
    pallas_call x1, Pallas kernels, pack_blocks(): pl.pallas_call(functools.partial(pack_kernel, block_cols), out_shape=jax....  8.04 us
    pallas_call x1, Pallas kernels, combine_blocks(): pl.pallas_call(combine_kernel, out_shape=jax.ShapeDtypeStruct(front.shape...  6.95 us
  transfers between devices with their start and end apart: 3, of which 1 were waited for; matrix products, arithmetic and copies ran while one was open for 4% of the time, Pallas kernels for 19%

profile of v1, /device:TPU:87, one launch (start us, length us, event | category | flops | bytes accessed | tf_op | source)
XLA Modules:
  0.0 321.1 jit_solution(9601773205136713389)
XLA Ops:
  7.4 0.0 all-reduce.2.cloned.1.call-start
  7.4 1.1 select_bitcast_fusion
  8.4 0.0 all-reduce.2.cloned.1.call-update
  8.5 0.0 all-gather.3.cloned.1.call-start
  8.5 0.5 all-gather.3.cloned.1.call-update
  9.7 0.0 copy-done.1
  9.7 0.1 fusion.3
  9.8 0.1 reduce_window_sum.26
  9.9 61.9 %shard_map.73 = f32[512,512]{1,0:T(8,128)} custom-call(f32[512,512]{1,0:T(8,128)} %bitcast.37), custom_call_target="tpu_custom_call" | custom-call | tf_op jit(solution)/shard_map/pallas_call | solution.py:190
  71.8 0.2 select_reduce_fusion
  72.0 1.3 scatter_custom_fusion.1.source_ref
  73.3 0.0 all-reduce.2.cloned.1.call-done
  73.3 3.4 %fusion.10 = f32[512,512]{1,0:T(8,128)S(1)} fusion(f32[512,512]{1,0:T(8,128)} %all-reduce.2.cloned.1.call-done, f32[512,512]{1,0:T(8,128)} %shard_map.73), kind=kOutput, calls=%fused_computation.24 | convolution fusion | flops 1610612736 | bytes 3145728 | tf_op jit(solution)/shard_map/dot_general | solution.py:24
  76.7 0.0 all-gather.3.cloned.1.call-done
  76.7 0.0 copy-start
  76.7 9.0 %fusion = f32[2048,512]{1,0:T(8,128)S(1)} fusion(f32[512,512]{1,0:T(8,128)} %shard_map.73, f32[1,2048,512]{2,1,0:T(8,128)} %all-gather.3.cloned.1.call-done), kind=kOutput, calls=%fused_computation.2 | convolution fusion | flops 6442450944 | bytes 9437184 | tf_op jit(solution)/shard_map/dot_general | solution.py:25
  85.7 0.0 copy-done
  85.7 8.5 %fusion.2.update_ref = f32[512,2048]{1,0:T(8,128)} fusion(f32[1,512,2048]{2,1,0:T(8,128)S(1)} %copy-done, f32[512,512]{1,0:T(8,128)S(1)} %fusion.10, f32[2048,512]{1,0:T(8,128)S(1)} %fusion, pred[2048]{0:T(1024)(128)(4,1)S(1)} %add_compare_fusion), kind=kOutput, calls=%fused_computation.5 | convolution fusion | flops 6444548096 | bytes 13633536 | tf_op jit(solution)/shard_map/dot_general | solution.py:26
  94.3 8.0 %shard_map.74 = f32[128,128,128]{2,1,0:T(8,128)} custom-call(s32[128]{0:T(128)} %scatter_custom_fusion.1.source_ref, f32[512,2048]{1,0:T(8,128)} %fusion.2.update_ref), custom_call_target="tpu_custom_call" | custom-call | tf_op jit(solution)/shard_map/pallas_call | solution.py:90
  102.3 10.1 %all-to-all-start = ((f32[16,1024,128]{2,1,0:T(8,128)}), f32[16,1024,128]{2,1,0:T(8,128)}, u32[]{:S(2)}, u32[]{:S(2)}) async-start(f32[16,1024,128]{2,1,0:T(8,128)} %bitcast.36), calls=%async_computation | async-start | bytes 16777216 | tf_op jit(solution)/shard_map/all_to_all | solution.py:55
  112.4 0.1 add.68
  112.5 0.1 add.69
  112.6 0.5 broadcast.100
  113.1 0.0 copy-done.2
  113.1 0.7 reduce.5
  113.8 0.1 reshape.111
  113.9 0.2 reduce_window_sum.24
  114.1 0.1 reduce_window_sum.25
  114.2 0.1 eq.38
  114.3 4.8 %scatter_custom_fusion.parent_ref = s32[128]{0:T(128)} fusion(s32[1024]{0:T(1024)S(1)} %bitcast.40, s32[1024]{0:T(1024)S(1)} %reshape.111, s32[]{:T(128)} %constant.12.clone.1), kind=kCustom, calls=%fused_computation.21 | custom fusion | bytes 516 | tf_op jit(solution)/shard_map/scatter | solution.py:69
  119.1 187.6 %all-to-all-done = f32[16,1024,128]{2,1,0:T(8,128)} async-done(((f32[16,1024,128]{2,1,0:T(8,128)}), f32[16,1024,128]{2,1,0:T(8,128)}, u32[]{:S(2)}, u32[]{:S(2)}) %all-to-all-start) | async-done | bytes 8388640 | tf_op jit(solution)/shard_map/all_to_all | solution.py:55
  306.7 6.9 %shard_map.75 = f32[128,2048]{1,0:T(8,128)} custom-call(s32[128]{0:T(128)} %scatter_custom_fusion.parent_ref, f32[128,128,128]{2,1,0:T(8,128)} %bitcast.12.incoming_ref, f32[128,2048]{1,0:T(8,128)} %bitcast.38), custom_call_target="tpu_custom_call" | custom-call | tf_op jit(solution)/shard_map/pallas_call | solution.py:118
  (9 shorter events, 0.1 us)
Async XLA Ops:
  7.4 2.3 copy-start.1
  7.4 65.9 %all-reduce.2.cloned.1.call-start = ((), (), s32[]{:S(2)}) async-start(), calls=%async_computation.1 | async-start | bytes 2097152 | tf_op jit(solution)/shard_map/psum | solution.py:15
  8.5 68.3 %all-gather.3.cloned.1.call-start = ((), (), s32[]{:S(2)}) async-start(), calls=%async_computation.2 | async-start | bytes 5242880 | tf_op jit(solution)/shard_map/all_gather | solution.py:21
  76.7 9.0 %copy-start = (f32[1,512,2048]{2,1,0:T(8,128)S(1)}, f32[1,512,2048]{2,1,0:T(8,128)}, u32[]{:S(2)}) copy-start(f32[1,512,2048]{2,1,0:T(8,128)} %param.9) | copy-start | bytes 12582916
  102.3 10.8 %copy-start.2 = (s32[16,1,1,64,1]{3,4,2,1,0:T(1,128)S(1)}, s32[16,1,1,64,1]{3,4,2,1,0:T(1,128)}, u32[]{:S(2)}) copy-start(s32[16,1,1,64,1]{3,4,2,1,0:T(1,128)} %param.13) | copy-start | bytes 12292
  102.3 204.4 %all-to-all-start = ((f32[16,1024,128]{2,1,0:T(8,128)}), f32[16,1024,128]{2,1,0:T(8,128)}, u32[]{:S(2)}, u32[]{:S(2)}) async-start(f32[16,1024,128]{2,1,0:T(8,128)} %bitcast.36), calls=%async_computation | async-start | bytes 16777216 | tf_op jit(solution)/shard_map/all_to_all | solution.py:55
Sparse Core Ops, SparseCore 0:
  10.9 49.0 all-reduce.1
Sparse Core Ops, SparseCore 1:
  10.9 52.8 all-gather.2

commit v2 on v0

--- a/solution.py
+++ b/solution.py
@@ -8,6 +8,7 @@
 from jax.sharding import PartitionSpec as P
 
 BS = 128
+STRIP = 32
 
 
 def spread(value, axis, root):
@@ -22,8 +23,8 @@
     chol_inv = factor_inverse(diag_block[0])
     contract_t = (((1,), (1,)), ((), ()))
     slab_factor = lax.dot_general(slab_rows, chol_inv, contract_t, precision=precise_mode)
-    col_factor = lax.dot_general(col_rows, chol_inv, contract_t, precision=precise_mode)
-    product = lax.dot_general(slab_factor, col_factor, contract_t, precision=precise_mode)
+    slab_solved = jnp.dot(slab_factor, chol_inv, precision=precise_mode)
+    product = lax.dot_general(slab_solved, col_rows, contract_t, precision=precise_mode)
     device_rows = trailing.shape[1]
     cols_dev = trailing.shape[2]
     column_ids = lax.axis_index("row") * cols_dev + jnp.arange(cols_dev, dtype=jnp.int32)
@@ -143,19 +144,33 @@
         g_ref[:, :BS] = work_ref[kk, kk]
         g_ref[:, BS:] = eye
 
-        def step(j, carry):
-            row = g_ref[pl.ds(j, 1), :]
-            pivot = jnp.sum(jnp.where(lane == j, row, 0.0), axis=1, keepdims=True)
-            scaled = row / jnp.sqrt(pivot)
-            down = jnp.where(lane[:, :BS] > j, scaled[:, :BS], 0.0)
-            down_col = jnp.transpose(jnp.broadcast_to(down, (BS, BS)))
-            g = g_ref[...]
-            g_ref[:, :BS] = g[:, :BS] - down_col * scaled[:, :BS]
-            g_ref[:, BS:] = g[:, BS:] - down_col * scaled[:, BS:]
-            g_ref[pl.ds(j, 1), :] = scaled
-            return carry
-
-        lax.fori_loop(0, BS, step, 0)
+        for strip in range(0, BS, STRIP):
+            for lo in range(strip, strip + STRIP, 8):
+                height = strip + STRIP - lo
+                rid = lo + lax.broadcasted_iota(jnp.int32, (height, 1), 0)
+
+                def step(j, carry, lo=lo, rid=rid, end=strip + STRIP):
+                    row = g_ref[pl.ds(j, 1), :]
+                    pivot = jnp.sum(jnp.where(lane == j, row, 0.0), axis=1, keepdims=True)
+                    inv_d = 1.0 / jnp.sqrt(pivot)
+                    scaled = row * inv_d
+                    live = g_ref[lo:end, :]
+                    column = jnp.sum(
+                        jnp.where(lane[:, :BS] == j, live[:, :BS], 0.0), axis=1, keepdims=True
+                    )
+                    down = jnp.where(rid > j, column * inv_d, 0.0)
+                    g_ref[lo:end, :] = live - down * scaled
+                    g_ref[pl.ds(j, 1), :] = scaled
+                    return carry
+
+                lax.fori_loop(lo, lo + 8, step, 0, unroll=2)
+            below = strip + STRIP
+            if below < BS:
+                done = g_ref[strip:below, :]
+                mult = jnp.transpose(done[:, :BS])[below:, :]
+                g_ref[below:, :] = g_ref[below:, :] - jnp.dot(
+                    mult, done, precision=hp, preferred_element_type=jnp.float32
+                )
         upper = jnp.where(col >= sub, g_ref[:, :BS], 0.0)
         lk_inv = g_ref[:, BS:]
         diag_inv.append(lk_inv)

time: 369 us -> 319 us (0.86)
  Pallas kernels: 124 us -> 78.6 us
  matrix products: 20.9 us -> 17.2 us
    pallas_call x1, Pallas kernels: 109 us -> 63.4 us  [factor_inverse(): pl.pallas_call(factor_kernel, out_shape=jax.ShapeDtypeStruct((n, n), a.dt...]
    dot_general x2, matrix products: 17.5 us -> 13.8 us  [the longest x1 10.8 us: shards(): lax.dot_general(slab_solved, col_rows, contract_t, precision=precise_mode)]
  transfers between devices with their start and end apart: 3 -> 3, of which waited for: 1 -> 1; matrix products, arithmetic and copies ran while one was open for 3% -> 5% of each run, Pallas kernels for 30% -> 20%
where the time goes in v2:
time: 319 us
  waiting for transfers between devices  188 us (59%)
  Pallas kernels  78.6 us (25%)
  matrix products  17.2 us (5%)
  between operations  15.6 us (5%)
  starting transfers between devices  10.2 us (3%)
  local copies, waits for them, and re-layouts  7 us (2%)
    all_to_all x1, waiting for transfers between devices, shards(): lax.all_to_all(outgoing.reshape(groups, capacity * BS, BS), 'cube', split...  188 us
    pallas_call x1, Pallas kernels, factor_inverse(): pl.pallas_call(factor_kernel, out_shape=jax.ShapeDtypeStruct((n, n), a.dt...  63.4 us
    dot_general x1, matrix products, shards(): lax.dot_general(slab_solved, col_rows, contract_t, precision=precise_mode)  10.8 us
    all_to_all x1, starting transfers between devices, shards(): lax.all_to_all(outgoing.reshape(groups, capacity * BS, BS), 'cube', split...  10.1 us
    pallas_call x1, Pallas kernels, pack_blocks(): pl.pallas_call(functools.partial(pack_kernel, block_cols), out_shape=jax....  8.04 us
    pallas_call x1, Pallas kernels, combine_blocks(): pl.pallas_call(combine_kernel, out_shape=jax.ShapeDtypeStruct(front.shape...  7.09 us
  transfers between devices with their start and end apart: 3, of which 1 were waited for; matrix products, arithmetic and copies ran while one was open for 5% of the time, Pallas kernels for 20%

profile of v2, /device:TPU:87, one launch (start us, length us, event | category | flops | bytes accessed | tf_op | source)
XLA Modules:
  0.0 319.1 jit_solution(16924576374373421373)
XLA Ops:
  7.4 0.0 copy-start
  7.4 0.0 all-reduce.2.cloned.1.call-start
  7.4 1.1 select_bitcast_fusion
  8.4 0.0 all-reduce.2.cloned.1.call-update
  8.5 0.0 all-gather.3.cloned.1.call-start
  8.5 0.5 all-gather.3.cloned.1.call-update
  9.7 0.0 copy-done
  9.7 0.1 fusion.5
  9.8 0.1 reduce_window_sum.26
  9.9 63.4 %shard_map.73 = f32[512,512]{1,0:T(8,128)} custom-call(f32[512,512]{1,0:T(8,128)} %bitcast.39), custom_call_target="tpu_custom_call" | custom-call | tf_op jit(solution)/shard_map/pallas_call | solution.py:199
  73.3 0.2 select_reduce_fusion
  73.5 1.3 scatter_custom_fusion.1.source_ref
  74.8 0.0 all-reduce.2.cloned.1.call-done
  74.8 3.4 %fusion.12 = f32[512,512]{1,0:T(8,128)S(1)} fusion(f32[512,512]{1,0:T(8,128)} %all-reduce.2.cloned.1.call-done, f32[512,512]{1,0:T(8,128)} %shard_map.73), kind=kOutput, calls=%fused_computation.24 | convolution fusion | flops 1610612736 | bytes 3145728 | tf_op jit(solution)/shard_map/dot_general | solution.py:25
  78.2 3.1 fusion.13
  81.3 0.0 all-gather.3.cloned.1.call-done
  81.4 10.8 %fusion.2.update_ref = f32[512,2048]{1,0:T(8,128)} fusion(f32[1,512,2048]{2,1,0:T(8,128)} %param.9, f32[512,512]{1,0:T(8,128)S(1)} %fusion.13, f32[1,2048,512]{2,1,0:T(8,128)} %all-gather.3.cloned.1.call-done, pred[2048]{0:T(1024)(128)(4,1)S(1)} %add_compare_fusion), kind=kOutput, calls=%fused_computation.5 | convolution fusion | flops 6444548096 | bytes 13633536 | tf_op jit(solution)/shard_map/dot_general | solution.py:27
  92.1 8.0 %shard_map.74 = f32[128,128,128]{2,1,0:T(8,128)} custom-call(s32[128]{0:T(128)} %scatter_custom_fusion.1.source_ref, f32[512,2048]{1,0:T(8,128)} %fusion.2.update_ref), custom_call_target="tpu_custom_call" | custom-call | tf_op jit(solution)/shard_map/pallas_call | solution.py:91
  100.2 0.0 copy-start.1
  100.2 10.1 %all-to-all-start = ((f32[16,1024,128]{2,1,0:T(8,128)}), f32[16,1024,128]{2,1,0:T(8,128)}, u32[]{:S(2)}, u32[]{:S(2)}) async-start(f32[16,1024,128]{2,1,0:T(8,128)} %bitcast.38), calls=%async_computation | async-start | bytes 16777216 | tf_op jit(solution)/shard_map/all_to_all | solution.py:56
  110.3 0.1 add.68
  110.4 0.1 add.69
  110.4 0.5 broadcast.100
  110.9 0.0 copy-done.1
  110.9 0.7 reduce.5
  111.6 0.1 reshape.111
  111.7 0.2 reduce_window_sum.24
  111.9 0.1 reduce_window_sum.25
  112.0 0.1 eq.38
  112.1 4.8 %scatter_custom_fusion.parent_ref = s32[128]{0:T(128)} fusion(s32[1024]{0:T(1024)S(1)} %bitcast.42, s32[1024]{0:T(1024)S(1)} %reshape.111, s32[]{:T(128)} %constant.12.clone.1), kind=kCustom, calls=%fused_computation.21 | custom fusion | bytes 516 | tf_op jit(solution)/shard_map/scatter | solution.py:70
  116.9 187.6 %all-to-all-done = f32[16,1024,128]{2,1,0:T(8,128)} async-done(((f32[16,1024,128]{2,1,0:T(8,128)}), f32[16,1024,128]{2,1,0:T(8,128)}, u32[]{:S(2)}, u32[]{:S(2)}) %all-to-all-start) | async-done | bytes 8388640 | tf_op jit(solution)/shard_map/all_to_all | solution.py:56
  304.6 7.1 %shard_map.75 = f32[128,2048]{1,0:T(8,128)} custom-call(s32[128]{0:T(128)} %scatter_custom_fusion.parent_ref, f32[128,128,128]{2,1,0:T(8,128)} %bitcast.12.incoming_ref, f32[128,2048]{1,0:T(8,128)} %bitcast.40), custom_call_target="tpu_custom_call" | custom-call | tf_op jit(solution)/shard_map/pallas_call | solution.py:119
  (7 shorter events, 0.1 us)
Async XLA Ops:
  7.4 2.3 copy-start
  7.4 67.5 %all-reduce.2.cloned.1.call-start = ((), (), s32[]{:S(2)}) async-start(), calls=%async_computation.1 | async-start | bytes 2097152 | tf_op jit(solution)/shard_map/psum | solution.py:16
  8.5 72.9 %all-gather.3.cloned.1.call-start = ((), (), s32[]{:S(2)}) async-start(), calls=%async_computation.2 | async-start | bytes 5242880 | tf_op jit(solution)/shard_map/all_gather | solution.py:22
  100.2 10.8 %copy-start.1 = (s32[16,1,1,64,1]{3,4,2,1,0:T(1,128)S(1)}, s32[16,1,1,64,1]{3,4,2,1,0:T(1,128)}, u32[]{:S(2)}) copy-start(s32[16,1,1,64,1]{3,4,2,1,0:T(1,128)} %param.13) | copy-start | bytes 12292
  100.2 204.4 %all-to-all-start = ((f32[16,1024,128]{2,1,0:T(8,128)}), f32[16,1024,128]{2,1,0:T(8,128)}, u32[]{:S(2)}, u32[]{:S(2)}) async-start(f32[16,1024,128]{2,1,0:T(8,128)} %bitcast.38), calls=%async_computation | async-start | bytes 16777216 | tf_op jit(solution)/shard_map/all_to_all | solution.py:56
Sparse Core Ops, SparseCore 0:
  10.9 49.1 all-reduce.1
Sparse Core Ops, SparseCore 1:
  10.9 53.0 all-gather.2

commit v3 on v2

--- a/solution.py
+++ b/solution.py
@@ -139,31 +139,22 @@
     col = lax.broadcasted_iota(jnp.int32, (BS, BS), 1)
     eye = (sub == col).astype(jnp.float32)
     diag_inv = []
+    rid = lax.broadcasted_iota(jnp.int32, (STRIP, 1), 0)
     for k in range(nb):
         kk = pl.ds(k * BS, BS)
         g_ref[:, :BS] = work_ref[kk, kk]
         g_ref[:, BS:] = eye
 
         for strip in range(0, BS, STRIP):
-            for lo in range(strip, strip + STRIP, 8):
-                height = strip + STRIP - lo
-                rid = lo + lax.broadcasted_iota(jnp.int32, (height, 1), 0)
-
-                def step(j, carry, lo=lo, rid=rid, end=strip + STRIP):
-                    row = g_ref[pl.ds(j, 1), :]
-                    pivot = jnp.sum(jnp.where(lane == j, row, 0.0), axis=1, keepdims=True)
-                    inv_d = 1.0 / jnp.sqrt(pivot)
-                    scaled = row * inv_d
-                    live = g_ref[lo:end, :]
-                    column = jnp.sum(
-                        jnp.where(lane[:, :BS] == j, live[:, :BS], 0.0), axis=1, keepdims=True
-                    )
-                    down = jnp.where(rid > j, column * inv_d, 0.0)
-                    g_ref[lo:end, :] = live - down * scaled
-                    g_ref[pl.ds(j, 1), :] = scaled
-                    return carry
-
-                lax.fori_loop(lo, lo + 8, step, 0, unroll=2)
+            held = g_ref[strip:strip + STRIP, :]
+            for local in range(STRIP):
+                j = strip + local
+                row = held[local:local + 1, :]
+                inv_d = 1.0 / jnp.sqrt(row[:, j:j + 1])
+                scaled = row * inv_d
+                down = jnp.where(rid > local, held[:, j:j + 1] * inv_d, 0.0)
+                held = jnp.where(rid == local, scaled, held - down * scaled)
+            g_ref[strip:strip + STRIP, :] = held
             below = strip + STRIP
             if below < BS:
                 done = g_ref[strip:below, :]

time: 319 us -> 313 us (0.981)
  Pallas kernels: 78.6 us -> 72.3 us
    pallas_call x1, Pallas kernels: 63.4 us -> 56.8 us  [factor_inverse(): pl.pallas_call(factor_kernel, out_shape=jax.ShapeDtypeStruct((n, n), a.dt...]
  transfers between devices with their start and end apart: 3 -> 3, of which waited for: 1 -> 1; matrix products, arithmetic and copies ran while one was open for 5% -> 5% of each run, Pallas kernels for 20% -> 18%
where the time goes in v3:
time: 313 us
  waiting for transfers between devices  188 us (60%)
  Pallas kernels  72.3 us (23%)
  matrix products  17.2 us (5%)
  between operations  15.6 us (5%)
  starting transfers between devices  10.1 us (3%)
  local copies, waits for them, and re-layouts  7 us (2%)
    all_to_all x1, waiting for transfers between devices, shards(): lax.all_to_all(outgoing.reshape(groups, capacity * BS, BS), 'cube', split...  188 us
    pallas_call x1, Pallas kernels, factor_inverse(): pl.pallas_call(factor_kernel, out_shape=jax.ShapeDtypeStruct((n, n), a.dt...  56.8 us
    dot_general x1, matrix products, shards(): lax.dot_general(slab_solved, col_rows, contract_t, precision=precise_mode)  10.8 us
    all_to_all x1, starting transfers between devices, shards(): lax.all_to_all(outgoing.reshape(groups, capacity * BS, BS), 'cube', split...  10.1 us
    pallas_call x1, Pallas kernels, pack_blocks(): pl.pallas_call(functools.partial(pack_kernel, block_cols), out_shape=jax....  8.04 us
    pallas_call x1, Pallas kernels, combine_blocks(): pl.pallas_call(combine_kernel, out_shape=jax.ShapeDtypeStruct(front.shape...  7.44 us
  transfers between devices with their start and end apart: 3, of which 1 were waited for; matrix products, arithmetic and copies ran while one was open for 5% of the time, Pallas kernels for 18%

profile of v3, /device:TPU:87, one launch (start us, length us, event | category | flops | bytes accessed | tf_op | source)
XLA Modules:
  0.0 312.8 jit_solution(12781449384127530058)
XLA Ops:
  7.4 0.0 copy-start
  7.4 0.0 all-reduce.2.cloned.1.call-start
  7.4 1.1 select_bitcast_fusion
  8.4 0.0 all-reduce.2.cloned.1.call-update
  8.5 0.0 all-gather.3.cloned.1.call-start
  8.5 0.5 all-gather.3.cloned.1.call-update
  9.7 0.0 copy-done
  9.7 0.1 fusion.5
  9.8 0.1 reduce_window_sum.26
  9.9 56.8 %shard_map.73 = f32[512,512]{1,0:T(8,128)} custom-call(f32[512,512]{1,0:T(8,128)} %bitcast.39), custom_call_target="tpu_custom_call" | custom-call | tf_op jit(solution)/shard_map/pallas_call | solution.py:190
  66.7 0.2 select_reduce_fusion
  66.9 1.3 scatter_custom_fusion.1.source_ref
  68.2 0.0 all-reduce.2.cloned.1.call-done
  68.2 3.4 %fusion.12 = f32[512,512]{1,0:T(8,128)S(1)} fusion(f32[512,512]{1,0:T(8,128)} %all-reduce.2.cloned.1.call-done, f32[512,512]{1,0:T(8,128)} %shard_map.73), kind=kOutput, calls=%fused_computation.24 | convolution fusion | flops 1610612736 | bytes 3145728 | tf_op jit(solution)/shard_map/dot_general | solution.py:25
  71.6 3.1 fusion.13
  74.7 0.0 all-gather.3.cloned.1.call-done
  74.7 10.8 %fusion.2.update_ref = f32[512,2048]{1,0:T(8,128)} fusion(f32[1,512,2048]{2,1,0:T(8,128)} %param.9, f32[512,512]{1,0:T(8,128)S(1)} %fusion.13, f32[1,2048,512]{2,1,0:T(8,128)} %all-gather.3.cloned.1.call-done, pred[2048]{0:T(1024)(128)(4,1)S(1)} %add_compare_fusion), kind=kOutput, calls=%fused_computation.5 | convolution fusion | flops 6444548096 | bytes 13633536 | tf_op jit(solution)/shard_map/dot_general | solution.py:27
  85.5 8.0 %shard_map.74 = f32[128,128,128]{2,1,0:T(8,128)} custom-call(s32[128]{0:T(128)} %scatter_custom_fusion.1.source_ref, f32[512,2048]{1,0:T(8,128)} %fusion.2.update_ref), custom_call_target="tpu_custom_call" | custom-call | tf_op jit(solution)/shard_map/pallas_call | solution.py:91
  93.5 0.0 copy-start.1
  93.5 10.1 %all-to-all-start = ((f32[16,1024,128]{2,1,0:T(8,128)}), f32[16,1024,128]{2,1,0:T(8,128)}, u32[]{:S(2)}, u32[]{:S(2)}) async-start(f32[16,1024,128]{2,1,0:T(8,128)} %bitcast.38), calls=%async_computation | async-start | bytes 16777216 | tf_op jit(solution)/shard_map/all_to_all | solution.py:56
  103.6 0.1 add.68
  103.7 0.1 add.69
  103.8 0.5 broadcast.100
  104.3 0.0 copy-done.1
  104.3 0.7 reduce.5
  105.0 0.1 reshape.111
  105.1 0.2 reduce_window_sum.24
  105.3 0.1 reduce_window_sum.25
  105.4 0.1 eq.38
  105.5 4.8 %scatter_custom_fusion.parent_ref = s32[128]{0:T(128)} fusion(s32[1024]{0:T(1024)S(1)} %bitcast.42, s32[1024]{0:T(1024)S(1)} %reshape.111, s32[]{:T(128)} %constant.12.clone.1), kind=kCustom, calls=%fused_computation.21 | custom fusion | bytes 516 | tf_op jit(solution)/shard_map/scatter | solution.py:70
  110.3 187.6 %all-to-all-done = f32[16,1024,128]{2,1,0:T(8,128)} async-done(((f32[16,1024,128]{2,1,0:T(8,128)}), f32[16,1024,128]{2,1,0:T(8,128)}, u32[]{:S(2)}, u32[]{:S(2)}) %all-to-all-start) | async-done | bytes 8388640 | tf_op jit(solution)/shard_map/all_to_all | solution.py:56
  297.9 7.4 %shard_map.75 = f32[128,2048]{1,0:T(8,128)} custom-call(s32[128]{0:T(128)} %scatter_custom_fusion.parent_ref, f32[128,128,128]{2,1,0:T(8,128)} %bitcast.12.incoming_ref, f32[128,2048]{1,0:T(8,128)} %bitcast.40), custom_call_target="tpu_custom_call" | custom-call | tf_op jit(solution)/shard_map/pallas_call | solution.py:119
  (7 shorter events, 0.1 us)
Async XLA Ops:
  7.4 2.3 copy-start
  7.4 60.8 %all-reduce.2.cloned.1.call-start = ((), (), s32[]{:S(2)}) async-start(), calls=%async_computation.1 | async-start | bytes 2097152 | tf_op jit(solution)/shard_map/psum | solution.py:16
  8.5 66.2 %all-gather.3.cloned.1.call-start = ((), (), s32[]{:S(2)}) async-start(), calls=%async_computation.2 | async-start | bytes 5242880 | tf_op jit(solution)/shard_map/all_gather | solution.py:22
  93.5 10.8 %copy-start.1 = (s32[16,1,1,64,1]{3,4,2,1,0:T(1,128)S(1)}, s32[16,1,1,64,1]{3,4,2,1,0:T(1,128)}, u32[]{:S(2)}) copy-start(s32[16,1,1,64,1]{3,4,2,1,0:T(1,128)} %param.13) | copy-start | bytes 12292
  93.5 204.4 %all-to-all-start = ((f32[16,1024,128]{2,1,0:T(8,128)}), f32[16,1024,128]{2,1,0:T(8,128)}, u32[]{:S(2)}, u32[]{:S(2)}) async-start(f32[16,1024,128]{2,1,0:T(8,128)} %bitcast.38), calls=%async_computation | async-start | bytes 16777216 | tf_op jit(solution)/shard_map/all_to_all | solution.py:56
Sparse Core Ops, SparseCore 0:
  10.9 49.0 all-reduce.1
Sparse Core Ops, SparseCore 1:
  10.9 52.9 all-gather.2

commit v4 on v3

--- a/solution.py
+++ b/solution.py
@@ -150,10 +150,12 @@
             for local in range(STRIP):
                 j = strip + local
                 row = held[local:local + 1, :]
-                inv_d = 1.0 / jnp.sqrt(row[:, j:j + 1])
-                scaled = row * inv_d
-                down = jnp.where(rid > local, held[:, j:j + 1] * inv_d, 0.0)
-                held = jnp.where(rid == local, scaled, held - down * scaled)
+                factor = jnp.where(rid > local, held[:, j:j + 1] / row[:, j:j + 1], 0.0)
+                held = held - factor * row
+            pivots = jnp.sum(
+                jnp.where(lane[:, :BS] == strip + rid, held[:, :BS], 0.0), axis=1, keepdims=True
+            )
+            held = held * (1.0 / jnp.sqrt(pivots))
             g_ref[strip:strip + STRIP, :] = held
             below = strip + STRIP
             if below < BS:

time: 313 us -> 307 us (0.981)
  Pallas kernels: 72.3 us -> 65.7 us
    pallas_call x1, Pallas kernels: 56.8 us -> 50.6 us  [factor_inverse(): pl.pallas_call(factor_kernel, out_shape=jax.ShapeDtypeStruct((n, n), a.dt...]
  transfers between devices with their start and end apart: 3 -> 3, of which waited for: 1 -> 1; matrix products, arithmetic and copies ran while one was open for 5% -> 5% of each run, Pallas kernels for 18% -> 17%
where the time goes in v4:
time: 307 us; the launch traced here: 306 us
  waiting for transfers between devices  188 us (61%)
  Pallas kernels  65.7 us (21%)
  matrix products  17.2 us (6%)
  between operations  15.6 us (5%)
  starting transfers between devices  10.2 us (3%)
  local copies, waits for them, and re-layouts  7 us (2%)
    all_to_all x1, waiting for transfers between devices, shards(): lax.all_to_all(outgoing.reshape(groups, capacity * BS, BS), 'cube', split...  188 us
    pallas_call x1, Pallas kernels, factor_inverse(): pl.pallas_call(factor_kernel, out_shape=jax.ShapeDtypeStruct((n, n), a.dt...  50.6 us
    dot_general x1, matrix products, shards(): lax.dot_general(slab_solved, col_rows, contract_t, precision=precise_mode)  10.8 us
    all_to_all x1, starting transfers between devices, shards(): lax.all_to_all(outgoing.reshape(groups, capacity * BS, BS), 'cube', split...  10.1 us
    pallas_call x1, Pallas kernels, pack_blocks(): pl.pallas_call(functools.partial(pack_kernel, block_cols), out_shape=jax....  8.04 us
    pallas_call x1, Pallas kernels, combine_blocks(): pl.pallas_call(combine_kernel, out_shape=jax.ShapeDtypeStruct(front.shape...  7.08 us
  transfers between devices with their start and end apart: 3, of which 1 were waited for; matrix products, arithmetic and copies ran while one was open for 5% of the time, Pallas kernels for 17%

profile of v4, /device:TPU:87, one launch (start us, length us, event | category | flops | bytes accessed | tf_op | source)
XLA Modules:
  0.0 306.2 jit_solution(6975660330066466942)
XLA Ops:
  7.4 0.0 copy-start
  7.4 0.0 all-reduce.2.cloned.1.call-start
  7.4 1.1 select_bitcast_fusion
  8.4 0.0 all-reduce.2.cloned.1.call-update
  8.5 0.0 all-gather.3.cloned.1.call-start
  8.5 0.5 all-gather.3.cloned.1.call-update
  9.7 0.0 copy-done
  9.7 0.1 fusion.5
  9.8 0.1 reduce_window_sum.26
  9.9 50.6 %shard_map.73 = f32[512,512]{1,0:T(8,128)} custom-call(f32[512,512]{1,0:T(8,128)} %bitcast.39), custom_call_target="tpu_custom_call" | custom-call | tf_op jit(solution)/shard_map/pallas_call | solution.py:192
  60.5 0.2 select_reduce_fusion
  60.7 1.3 scatter_custom_fusion.1.source_ref
  62.0 0.0 all-reduce.2.cloned.1.call-done
  62.0 3.4 %fusion.12 = f32[512,512]{1,0:T(8,128)S(1)} fusion(f32[512,512]{1,0:T(8,128)} %all-reduce.2.cloned.1.call-done, f32[512,512]{1,0:T(8,128)} %shard_map.73), kind=kOutput, calls=%fused_computation.24 | convolution fusion | flops 1610612736 | bytes 3145728 | tf_op jit(solution)/shard_map/dot_general | solution.py:25
  65.4 3.1 %fusion.13 = f32[512,512]{1,0:T(8,128)S(1)} fusion(f32[512,512]{1,0:T(8,128)S(1)} %fusion.12, f32[512,512]{1,0:T(8,128)} %shard_map.73), kind=kOutput, calls=%fused_computation.25 | convolution fusion | flops 1610612736 | bytes 3145728 | tf_op jit(solution)/shard_map/dot_general | solution.py:26
  68.5 0.0 all-gather.3.cloned.1.call-done
  68.5 10.8 %fusion.2.update_ref = f32[512,2048]{1,0:T(8,128)} fusion(f32[1,512,2048]{2,1,0:T(8,128)} %param.9, f32[512,512]{1,0:T(8,128)S(1)} %fusion.13, f32[1,2048,512]{2,1,0:T(8,128)} %all-gather.3.cloned.1.call-done, pred[2048]{0:T(1024)(128)(4,1)S(1)} %add_compare_fusion), kind=kOutput, calls=%fused_computation.5 | convolution fusion | flops 6444548096 | bytes 13633536 | tf_op jit(solution)/shard_map/dot_general | solution.py:27
  79.3 8.0 %shard_map.74 = f32[128,128,128]{2,1,0:T(8,128)} custom-call(s32[128]{0:T(128)} %scatter_custom_fusion.1.source_ref, f32[512,2048]{1,0:T(8,128)} %fusion.2.update_ref), custom_call_target="tpu_custom_call" | custom-call | tf_op jit(solution)/shard_map/pallas_call | solution.py:91
  87.3 0.0 copy-start.1
  87.3 10.1 %all-to-all-start = ((f32[16,1024,128]{2,1,0:T(8,128)}), f32[16,1024,128]{2,1,0:T(8,128)}, u32[]{:S(2)}, u32[]{:S(2)}) async-start(f32[16,1024,128]{2,1,0:T(8,128)} %bitcast.38), calls=%async_computation | async-start | bytes 16777216 | tf_op jit(solution)/shard_map/all_to_all | solution.py:56
  97.4 0.1 add.68
  97.5 0.1 add.69
  97.6 0.5 broadcast.100
  98.1 0.0 copy-done.1
  98.1 0.7 reduce.5
  98.8 0.1 reshape.111
  98.9 0.2 reduce_window_sum.24
  99.1 0.1 reduce_window_sum.25
  99.2 0.1 eq.38
  99.3 4.8 %scatter_custom_fusion.parent_ref = s32[128]{0:T(128)} fusion(s32[1024]{0:T(1024)S(1)} %bitcast.42, s32[1024]{0:T(1024)S(1)} %reshape.111, s32[]{:T(128)} %constant.12.clone.1), kind=kCustom, calls=%fused_computation.21 | custom fusion | bytes 516 | tf_op jit(solution)/shard_map/scatter | solution.py:70
  104.1 187.6 %all-to-all-done = f32[16,1024,128]{2,1,0:T(8,128)} async-done(((f32[16,1024,128]{2,1,0:T(8,128)}), f32[16,1024,128]{2,1,0:T(8,128)}, u32[]{:S(2)}, u32[]{:S(2)}) %all-to-all-start) | async-done | bytes 8388640 | tf_op jit(solution)/shard_map/all_to_all | solution.py:56
  291.7 7.1 %shard_map.75 = f32[128,2048]{1,0:T(8,128)} custom-call(s32[128]{0:T(128)} %scatter_custom_fusion.parent_ref, f32[128,128,128]{2,1,0:T(8,128)} %bitcast.12.incoming_ref, f32[128,2048]{1,0:T(8,128)} %bitcast.40), custom_call_target="tpu_custom_call" | custom-call | tf_op jit(solution)/shard_map/pallas_call | solution.py:119
  (7 shorter events, 0.1 us)
Async XLA Ops:
  7.4 2.3 copy-start
  7.4 54.6 %all-reduce.2.cloned.1.call-start = ((), (), s32[]{:S(2)}) async-start(), calls=%async_computation.1 | async-start | bytes 2097152 | tf_op jit(solution)/shard_map/psum | solution.py:16
  8.5 60.0 %all-gather.3.cloned.1.call-start = ((), (), s32[]{:S(2)}) async-start(), calls=%async_computation.2 | async-start | bytes 5242880 | tf_op jit(solution)/shard_map/all_gather | solution.py:22
  87.3 10.8 %copy-start.1 = (s32[16,1,1,64,1]{3,4,2,1,0:T(1,128)S(1)}, s32[16,1,1,64,1]{3,4,2,1,0:T(1,128)}, u32[]{:S(2)}) copy-start(s32[16,1,1,64,1]{3,4,2,1,0:T(1,128)} %param.13) | copy-start | bytes 12292
  87.3 204.4 %all-to-all-start = ((f32[16,1024,128]{2,1,0:T(8,128)}), f32[16,1024,128]{2,1,0:T(8,128)}, u32[]{:S(2)}, u32[]{:S(2)}) async-start(f32[16,1024,128]{2,1,0:T(8,128)} %bitcast.38), calls=%async_computation | async-start | bytes 16777216 | tf_op jit(solution)/shard_map/all_to_all | solution.py:56
Sparse Core Ops, SparseCore 0:
  10.9 48.9 all-reduce.1
Sparse Core Ops, SparseCore 1:
  10.9 53.0 all-gather.2

commit v5 on v4

--- a/solution.py
+++ b/solution.py
@@ -22,9 +22,10 @@
     col_rows = lax.all_gather(panel[0], "col", axis=0, tiled=True)
     chol_inv = factor_inverse(diag_block[0])
     contract_t = (((1,), (1,)), ((), ()))
-    slab_factor = lax.dot_general(slab_rows, chol_inv, contract_t, precision=precise_mode)
-    slab_solved = jnp.dot(slab_factor, chol_inv, precision=precise_mode)
-    product = lax.dot_general(slab_solved, col_rows, contract_t, precision=precise_mode)
+    split_mode = lax.Precision.HIGH
+    slab_factor = lax.dot_general(slab_rows, chol_inv, contract_t, precision=split_mode)
+    slab_solved = jnp.dot(slab_factor, chol_inv, precision=split_mode)
+    product = lax.dot_general(slab_solved, col_rows, contract_t, precision=split_mode)
     device_rows = trailing.shape[1]
     cols_dev = trailing.shape[2]
     column_ids = lax.axis_index("row") * cols_dev + jnp.arange(cols_dev, dtype=jnp.int32)

time: 307 us -> 302 us (0.984)
  matrix products: 17.2 us -> 12.7 us
    dot_general x3, matrix products: 17.2 us -> 12.7 us  [the longest x1 7.94 us: shards(): lax.dot_general(slab_solved, col_rows, contract_t, precision=split_mode)]
  transfers between devices with their start and end apart: 3 -> 3, of which waited for: 1 -> 1; matrix products, arithmetic and copies ran while one was open for 5% -> 4% of each run, Pallas kernels for 17% -> 17%
where the time goes in v5:
time: 302 us
  waiting for transfers between devices  188 us (62%)
  Pallas kernels  65.5 us (22%)
  between operations  15.6 us (5%)
  matrix products  12.7 us (4%)
  starting transfers between devices  10.2 us (3%)
  local copies, waits for them, and re-layouts  7 us (2%)
    all_to_all x1, waiting for transfers between devices, shards(): lax.all_to_all(outgoing.reshape(groups, capacity * BS, BS), 'cube', split...  188 us
    pallas_call x1, Pallas kernels, factor_inverse(): pl.pallas_call(factor_kernel, out_shape=jax.ShapeDtypeStruct((n, n), a.dt...  50.6 us
    all_to_all x1, starting transfers between devices, shards(): lax.all_to_all(outgoing.reshape(groups, capacity * BS, BS), 'cube', split...  10.1 us
    pallas_call x1, Pallas kernels, pack_blocks(): pl.pallas_call(functools.partial(pack_kernel, block_cols), out_shape=jax....  8.04 us
    dot_general x1, matrix products, shards(): lax.dot_general(slab_solved, col_rows, contract_t, precision=split_mode)  7.94 us
    pallas_call x1, Pallas kernels, combine_blocks(): pl.pallas_call(combine_kernel, out_shape=jax.ShapeDtypeStruct(front.shape...  6.9 us
  transfers between devices with their start and end apart: 3, of which 1 were waited for; matrix products, arithmetic and copies ran while one was open for 4% of the time, Pallas kernels for 17%

profile of v5, /device:TPU:87, one launch (start us, length us, event | category | flops | bytes accessed | tf_op | source)
XLA Modules:
  0.0 301.6 jit_solution(1715512995663122709)
XLA Ops:
  7.4 0.0 copy-start
  7.4 0.0 all-reduce.2.cloned.1.call-start
  7.4 1.1 select_bitcast_fusion
  8.4 0.0 all-reduce.2.cloned.1.call-update
  8.5 0.0 all-gather.3.cloned.1.call-start
  8.5 0.5 all-gather.3.cloned.1.call-update
  9.7 0.0 copy-done
  9.7 0.1 fusion.5
  9.8 0.1 reduce_window_sum.26
  9.9 50.6 %shard_map.73 = f32[512,512]{1,0:T(8,128)} custom-call(f32[512,512]{1,0:T(8,128)} %bitcast.39), custom_call_target="tpu_custom_call" | custom-call | tf_op jit(solution)/shard_map/pallas_call | solution.py:193
  60.5 0.2 select_reduce_fusion
  60.7 1.3 scatter_custom_fusion.1.source_ref
  62.0 0.0 all-reduce.2.cloned.1.call-done
  62.0 2.6 fusion.12
  64.6 2.2 fusion.13
  66.8 0.0 all-gather.3.cloned.1.call-done
  66.8 7.9 %fusion.2.update_ref = f32[512,2048]{1,0:T(8,128)} fusion(f32[1,512,2048]{2,1,0:T(8,128)} %param.9, f32[512,512]{1,0:T(8,128)S(1)} %fusion.13, f32[1,2048,512]{2,1,0:T(8,128)} %all-gather.3.cloned.1.call-done, pred[2048]{0:T(1024)(128)(4,1)S(1)} %add_compare_fusion), kind=kOutput, calls=%fused_computation.5 | convolution fusion | flops 3223322624 | bytes 13633536 | tf_op jit(solution)/shard_map/dot_general | solution.py:28
  74.8 8.0 %shard_map.74 = f32[128,128,128]{2,1,0:T(8,128)} custom-call(s32[128]{0:T(128)} %scatter_custom_fusion.1.source_ref, f32[512,2048]{1,0:T(8,128)} %fusion.2.update_ref), custom_call_target="tpu_custom_call" | custom-call | tf_op jit(solution)/shard_map/pallas_call | solution.py:92
  82.8 0.0 copy-start.1
  82.8 10.1 %all-to-all-start = ((f32[16,1024,128]{2,1,0:T(8,128)}), f32[16,1024,128]{2,1,0:T(8,128)}, u32[]{:S(2)}, u32[]{:S(2)}) async-start(f32[16,1024,128]{2,1,0:T(8,128)} %bitcast.38), calls=%async_computation | async-start | bytes 16777216 | tf_op jit(solution)/shard_map/all_to_all | solution.py:57
  92.9 0.1 add.68
  93.0 0.1 add.69
  93.1 0.5 broadcast.100
  93.6 0.0 copy-done.1
  93.6 0.7 reduce.5
  94.3 0.1 reshape.111
  94.4 0.2 reduce_window_sum.24
  94.6 0.1 reduce_window_sum.25
  94.7 0.1 eq.38
  94.8 4.8 %scatter_custom_fusion.parent_ref = s32[128]{0:T(128)} fusion(s32[1024]{0:T(1024)S(1)} %bitcast.42, s32[1024]{0:T(1024)S(1)} %reshape.111, s32[]{:T(128)} %constant.12.clone.1), kind=kCustom, calls=%fused_computation.21 | custom fusion | bytes 516 | tf_op jit(solution)/shard_map/scatter | solution.py:71
  99.6 187.6 %all-to-all-done = f32[16,1024,128]{2,1,0:T(8,128)} async-done(((f32[16,1024,128]{2,1,0:T(8,128)}), f32[16,1024,128]{2,1,0:T(8,128)}, u32[]{:S(2)}, u32[]{:S(2)}) %all-to-all-start) | async-done | bytes 8388640 | tf_op jit(solution)/shard_map/all_to_all | solution.py:57
  287.2 6.9 %shard_map.75 = f32[128,2048]{1,0:T(8,128)} custom-call(s32[128]{0:T(128)} %scatter_custom_fusion.parent_ref, f32[128,128,128]{2,1,0:T(8,128)} %bitcast.12.incoming_ref, f32[128,2048]{1,0:T(8,128)} %bitcast.40), custom_call_target="tpu_custom_call" | custom-call | tf_op jit(solution)/shard_map/pallas_call | solution.py:120
  (7 shorter events, 0.1 us)
Async XLA Ops:
  7.4 2.3 copy-start
  7.4 54.6 %all-reduce.2.cloned.1.call-start = ((), (), s32[]{:S(2)}) async-start(), calls=%async_computation.1 | async-start | bytes 2097152 | tf_op jit(solution)/shard_map/psum | solution.py:16
  8.5 58.4 %all-gather.3.cloned.1.call-start = ((), (), s32[]{:S(2)}) async-start(), calls=%async_computation.2 | async-start | bytes 5242880 | tf_op jit(solution)/shard_map/all_gather | solution.py:22
  82.8 10.8 %copy-start.1 = (s32[16,1,1,64,1]{3,4,2,1,0:T(1,128)S(1)}, s32[16,1,1,64,1]{3,4,2,1,0:T(1,128)}, u32[]{:S(2)}) copy-start(s32[16,1,1,64,1]{3,4,2,1,0:T(1,128)} %param.13) | copy-start | bytes 12292
  82.8 204.4 %all-to-all-start = ((f32[16,1024,128]{2,1,0:T(8,128)}), f32[16,1024,128]{2,1,0:T(8,128)}, u32[]{:S(2)}, u32[]{:S(2)}) async-start(f32[16,1024,128]{2,1,0:T(8,128)} %bitcast.38), calls=%async_computation | async-start | bytes 16777216 | tf_op jit(solution)/shard_map/all_to_all | solution.py:57
Sparse Core Ops, SparseCore 0:
  10.9 48.9 all-reduce.1
Sparse Core Ops, SparseCore 1:
  10.9 53.0 all-gather.2

commit v6 on v5

--- a/solution.py
+++ b/solution.py
@@ -74,17 +74,33 @@
     return assembled[None]
 
 
-def pack_kernel(block_cols, source_ref, update_ref, out_ref):
-    def body(slot, carry):
+def pack_kernel(block_cols, source_ref, update_ref, out_ref, sems):
+    nslots = out_ref.shape[0]
+
+    def start(slot, carry):
         block = source_ref[slot]
-        live = block >= 0
-        block = jnp.maximum(block, 0)
-        rows = pl.ds(pl.multiple_of((block // block_cols) * BS, BS), BS)
-        cols = pl.ds(pl.multiple_of((block % block_cols) * BS, BS), BS)
-        out_ref[slot] = jnp.where(live, update_ref[rows, cols], jnp.float32(0.0))
+
+        @pl.when(block >= 0)
+        def _():
+            rows = pl.ds(pl.multiple_of((block // block_cols) * BS, BS), BS)
+            cols = pl.ds(pl.multiple_of((block % block_cols) * BS, BS), BS)
+            pltpu.make_async_copy(update_ref.at[rows, cols], out_ref.at[slot], sems.at[slot]).start()
+
         return carry
 
-    lax.fori_loop(0, out_ref.shape[0], body, 0)
+    def finish(slot, carry):
+        block = source_ref[slot]
+
+        @pl.when(block >= 0)
+        def _():
+            pltpu.make_async_copy(
+                update_ref.at[pl.ds(0, BS), pl.ds(0, BS)], out_ref.at[slot], sems.at[slot]
+            ).wait()
+
+        return carry
+
+    lax.fori_loop(0, nslots, start, 0)
+    lax.fori_loop(0, nslots, finish, 0)
 
 
 def pack_blocks(source_of_slot, update, block_cols):
@@ -96,7 +112,8 @@
             pl.BlockSpec(memory_space=pltpu.SMEM),
             pl.BlockSpec(memory_space=pltpu.VMEM),
         ],
-        out_specs=pl.BlockSpec(memory_space=pltpu.VMEM),
+        out_specs=pl.BlockSpec(memory_space=pl.ANY),
+        scratch_shapes=[pltpu.SemaphoreType.DMA((nslots,))],
     )(source_of_slot, update)
 
 

time: 302 us -> 301 us (level)
  no operation moved by 1% of the time
where the time goes in v6:
time: 301 us; the launch traced here: 300 us
  waiting for transfers between devices  188 us (62%)
  Pallas kernels  64.5 us (21%)
  between operations  15.6 us (5%)
  matrix products  12.7 us (4%)
  starting transfers between devices  10 us (3%)
  local copies, waits for them, and re-layouts  7 us (2%)
    all_to_all x1, waiting for transfers between devices, shards(): lax.all_to_all(outgoing.reshape(groups, capacity * BS, BS), 'cube', split...  188 us
    pallas_call x1, Pallas kernels, factor_inverse(): pl.pallas_call(factor_kernel, out_shape=jax.ShapeDtypeStruct((n, n), a.dt...  50.6 us
    all_to_all x1, starting transfers between devices, shards(): lax.all_to_all(outgoing.reshape(groups, capacity * BS, BS), 'cube', split...  9.99 us
    dot_general x1, matrix products, shards(): lax.dot_general(slab_solved, col_rows, contract_t, precision=split_mode)  7.94 us
    pallas_call x1, Pallas kernels, combine_blocks(): pl.pallas_call(combine_kernel, out_shape=jax.ShapeDtypeStruct(front.shape...  7.52 us
    pallas_call x1, Pallas kernels, pack_blocks(): pl.pallas_call(functools.partial(pack_kernel, block_cols), out_shape=jax....  6.37 us
  transfers between devices with their start and end apart: 3, of which 1 were waited for; matrix products, arithmetic and copies ran while one was open for 4% of the time, Pallas kernels for 17%

profile of v6, /device:TPU:87, one launch (start us, length us, event | category | flops | bytes accessed | tf_op | source)
XLA Modules:
  0.0 300.4 jit_solution(5734130161008318439)
XLA Ops:
  7.4 0.0 copy-start
  7.4 0.0 all-reduce.2.cloned.1.call-start
  7.4 1.1 select_bitcast_fusion
  8.4 0.0 all-reduce.2.cloned.1.call-update
  8.5 0.0 all-gather.3.cloned.1.call-start
  8.5 0.5 all-gather.3.cloned.1.call-update
  9.7 0.0 copy-done
  9.7 0.1 fusion.5
  9.8 0.1 reduce_window_sum.26
  9.9 50.6 %shard_map.73 = f32[512,512]{1,0:T(8,128)} custom-call(f32[512,512]{1,0:T(8,128)} %bitcast.39), custom_call_target="tpu_custom_call" | custom-call | tf_op jit(solution)/shard_map/pallas_call | solution.py:210
  60.5 0.2 select_reduce_fusion
  60.7 1.3 scatter_custom_fusion.1.source_ref
  62.0 0.0 all-reduce.2.cloned.1.call-done
  62.0 2.6 fusion.12
  64.6 2.2 fusion.13
  66.8 0.0 all-gather.3.cloned.1.call-done
  66.8 7.9 %fusion.2.update_ref = f32[512,2048]{1,0:T(8,128)} fusion(f32[1,512,2048]{2,1,0:T(8,128)} %param.9, f32[512,512]{1,0:T(8,128)S(1)} %fusion.13, f32[1,2048,512]{2,1,0:T(8,128)} %all-gather.3.cloned.1.call-done, pred[2048]{0:T(1024)(128)(4,1)S(1)} %add_compare_fusion), kind=kOutput, calls=%fused_computation.5 | convolution fusion | flops 3223322624 | bytes 13633536 | tf_op jit(solution)/shard_map/dot_general | solution.py:28
  74.8 6.4 %shard_map.74 = f32[128,128,128]{2,1,0:T(8,128)} custom-call(s32[128]{0:T(128)} %scatter_custom_fusion.1.source_ref, f32[512,2048]{1,0:T(8,128)} %fusion.2.update_ref), custom_call_target="tpu_custom_call" | custom-call | tf_op jit(solution)/shard_map/pallas_call | solution.py:108
  81.1 0.0 copy-start.1
  81.2 10.0 %all-to-all-start = ((f32[16,1024,128]{2,1,0:T(8,128)}), f32[16,1024,128]{2,1,0:T(8,128)}, u32[]{:S(2)}, u32[]{:S(2)}) async-start(f32[16,1024,128]{2,1,0:T(8,128)} %bitcast.38), calls=%async_computation | async-start | bytes 16777216 | tf_op jit(solution)/shard_map/all_to_all | solution.py:57
  91.2 0.1 add.68
  91.2 0.1 add.69
  91.3 0.5 broadcast.100
  91.8 0.0 copy-done.1
  91.8 0.7 reduce.5
  92.5 0.1 reshape.111
  92.6 0.2 reduce_window_sum.24
  92.8 0.1 reduce_window_sum.25
  92.9 0.1 eq.38
  93.0 4.8 %scatter_custom_fusion.parent_ref = s32[128]{0:T(128)} fusion(s32[1024]{0:T(1024)S(1)} %bitcast.42, s32[1024]{0:T(1024)S(1)} %reshape.111, s32[]{:T(128)} %constant.12.clone.1), kind=kCustom, calls=%fused_computation.21 | custom fusion | bytes 516 | tf_op jit(solution)/shard_map/scatter | solution.py:71
  97.8 187.6 %all-to-all-done = f32[16,1024,128]{2,1,0:T(8,128)} async-done(((f32[16,1024,128]{2,1,0:T(8,128)}), f32[16,1024,128]{2,1,0:T(8,128)}, u32[]{:S(2)}, u32[]{:S(2)}) %all-to-all-start) | async-done | bytes 8388640 | tf_op jit(solution)/shard_map/all_to_all | solution.py:57
  285.4 7.5 %shard_map.75 = f32[128,2048]{1,0:T(8,128)} custom-call(s32[128]{0:T(128)} %scatter_custom_fusion.parent_ref, f32[128,128,128]{2,1,0:T(8,128)} %bitcast.12.incoming_ref, f32[128,2048]{1,0:T(8,128)} %bitcast.40), custom_call_target="tpu_custom_call" | custom-call | tf_op jit(solution)/shard_map/pallas_call | solution.py:137
  (7 shorter events, 0.1 us)
Async XLA Ops:
  7.4 2.3 copy-start
  7.4 54.6 %all-reduce.2.cloned.1.call-start = ((), (), s32[]{:S(2)}) async-start(), calls=%async_computation.1 | async-start | bytes 2097152 | tf_op jit(solution)/shard_map/psum | solution.py:16
  8.5 58.4 %all-gather.3.cloned.1.call-start = ((), (), s32[]{:S(2)}) async-start(), calls=%async_computation.2 | async-start | bytes 5242880 | tf_op jit(solution)/shard_map/all_gather | solution.py:22
  81.1 10.7 %copy-start.1 = (s32[16,1,1,64,1]{3,4,2,1,0:T(1,128)S(1)}, s32[16,1,1,64,1]{3,4,2,1,0:T(1,128)}, u32[]{:S(2)}) copy-start(s32[16,1,1,64,1]{3,4,2,1,0:T(1,128)} %param.13) | copy-start | bytes 12292
  81.2 204.3 %all-to-all-start = ((f32[16,1024,128]{2,1,0:T(8,128)}), f32[16,1024,128]{2,1,0:T(8,128)}, u32[]{:S(2)}, u32[]{:S(2)}) async-start(f32[16,1024,128]{2,1,0:T(8,128)} %bitcast.38), calls=%async_computation | async-start | bytes 16777216 | tf_op jit(solution)/shard_map/all_to_all | solution.py:57
Sparse Core Ops, SparseCore 0:
  10.9 48.9 all-reduce.1
Sparse Core Ops, SparseCore 1:
  10.9 53.0 all-gather.2

commit v7 on v6

--- a/solution.py
+++ b/solution.py
@@ -117,7 +117,17 @@
     )(source_of_slot, update)
 
 
-def combine_kernel(parent_ref, incoming_ref, front_ref, out_ref):
+def combine_kernel(parent_ref, incoming_ref, front_ref, out_ref, landed, sems):
+    nslots = incoming_ref.shape[0]
+
+    def start(slot, carry):
+        @pl.when(parent_ref[slot] >= 0)
+        def _():
+            pltpu.make_async_copy(incoming_ref.at[slot], landed.at[slot], sems.at[slot]).start()
+
+        return carry
+
+    lax.fori_loop(0, nslots, start, 0)
     out_ref[...] = front_ref[...]
 
     def body(slot, carry):
@@ -125,24 +135,30 @@
 
         @pl.when(parent >= 0)
         def _():
+            pltpu.make_async_copy(incoming_ref.at[slot], landed.at[slot], sems.at[slot]).wait()
             cols = pl.ds(pl.multiple_of(parent * BS, BS), BS)
-            out_ref[:, cols] = out_ref[:, cols] + incoming_ref[slot]
-
-        return carry
-
-    lax.fori_loop(0, incoming_ref.shape[0], body, 0)
+            out_ref[:, cols] = out_ref[:, cols] + landed[slot]
+
+        return carry
+
+    lax.fori_loop(0, nslots, body, 0)
 
 
 def combine_blocks(parent_of_slot, incoming, front):
+    nslots = incoming.shape[0]
     return pl.pallas_call(
         combine_kernel,
         out_shape=jax.ShapeDtypeStruct(front.shape, front.dtype),
         in_specs=[
             pl.BlockSpec(memory_space=pltpu.SMEM),
-            pl.BlockSpec(memory_space=pltpu.VMEM),
+            pl.BlockSpec(memory_space=pl.ANY),
             pl.BlockSpec(memory_space=pltpu.VMEM),
         ],
         out_specs=pl.BlockSpec(memory_space=pltpu.VMEM),
+        scratch_shapes=[
+            pltpu.VMEM((nslots, BS, BS), incoming.dtype),
+            pltpu.SemaphoreType.DMA((nslots,)),
+        ],
     )(parent_of_slot, incoming, front)
 
 

time: 301 us -> 301 us (level)
  no operation moved by 1% of the time
where the time goes in v7:
time: 301 us; the launch traced here: 300 us
  waiting for transfers between devices  188 us (62%)
  Pallas kernels  64.3 us (21%)
  between operations  15.6 us (5%)
  matrix products  12.7 us (4%)
  starting transfers between devices  10 us (3%)
  local copies, waits for them, and re-layouts  7 us (2%)
    all_to_all x1, waiting for transfers between devices, shards(): lax.all_to_all(outgoing.reshape(groups, capacity * BS, BS), 'cube', split...  188 us
    pallas_call x1, Pallas kernels, factor_inverse(): pl.pallas_call(factor_kernel, out_shape=jax.ShapeDtypeStruct((n, n), a.dt...  50.6 us
    all_to_all x1, starting transfers between devices, shards(): lax.all_to_all(outgoing.reshape(groups, capacity * BS, BS), 'cube', split...  9.99 us
    dot_general x1, matrix products, shards(): lax.dot_general(slab_solved, col_rows, contract_t, precision=split_mode)  7.94 us
    pallas_call x1, Pallas kernels, combine_blocks(): pl.pallas_call(combine_kernel, out_shape=jax.ShapeDtypeStruct(front.shape...  7.37 us
    pallas_call x1, Pallas kernels, pack_blocks(): pl.pallas_call(functools.partial(pack_kernel, block_cols), out_shape=jax....  6.37 us
  transfers between devices with their start and end apart: 3, of which 1 were waited for; matrix products, arithmetic and copies ran while one was open for 4% of the time, Pallas kernels for 17%

profile of v7, /device:TPU:87, one launch (start us, length us, event | category | flops | bytes accessed | tf_op | source)
XLA Modules:
  0.0 300.3 jit_solution(139959206567794094)
XLA Ops:
  7.4 0.0 copy-start
  7.4 0.0 all-reduce.2.cloned.1.call-start
  7.4 1.1 select_bitcast_fusion
  8.4 0.0 all-reduce.2.cloned.1.call-update
  8.5 0.0 all-gather.3.cloned.1.call-start
  8.5 0.5 all-gather.3.cloned.1.call-update
  9.7 0.0 copy-done
  9.7 0.1 fusion.5
  9.8 0.1 reduce_window_sum.26
  9.9 50.6 %shard_map.73 = f32[512,512]{1,0:T(8,128)} custom-call(f32[512,512]{1,0:T(8,128)} %bitcast.39), custom_call_target="tpu_custom_call" | custom-call | tf_op jit(solution)/shard_map/pallas_call | solution.py:226
  60.5 0.2 select_reduce_fusion
  60.7 1.3 scatter_custom_fusion.1.source_ref
  62.0 0.0 all-reduce.2.cloned.1.call-done
  62.0 2.6 fusion.12
  64.6 2.2 fusion.13
  66.8 0.0 all-gather.3.cloned.1.call-done
  66.8 7.9 %fusion.2.update_ref = f32[512,2048]{1,0:T(8,128)} fusion(f32[1,512,2048]{2,1,0:T(8,128)} %param.9, f32[512,512]{1,0:T(8,128)S(1)} %fusion.13, f32[1,2048,512]{2,1,0:T(8,128)} %all-gather.3.cloned.1.call-done, pred[2048]{0:T(1024)(128)(4,1)S(1)} %add_compare_fusion), kind=kOutput, calls=%fused_computation.5 | convolution fusion | flops 3223322624 | bytes 13633536 | tf_op jit(solution)/shard_map/dot_general | solution.py:28
  74.8 6.4 %shard_map.74 = f32[128,128,128]{2,1,0:T(8,128)} custom-call(s32[128]{0:T(128)} %scatter_custom_fusion.1.source_ref, f32[512,2048]{1,0:T(8,128)} %fusion.2.update_ref), custom_call_target="tpu_custom_call" | custom-call | tf_op jit(solution)/shard_map/pallas_call | solution.py:108
  81.1 0.0 copy-start.1
  81.2 10.0 %all-to-all-start = ((f32[16,1024,128]{2,1,0:T(8,128)}), f32[16,1024,128]{2,1,0:T(8,128)}, u32[]{:S(2)}, u32[]{:S(2)}) async-start(f32[16,1024,128]{2,1,0:T(8,128)} %bitcast.38), calls=%async_computation | async-start | bytes 16777216 | tf_op jit(solution)/shard_map/all_to_all | solution.py:57
  91.2 0.1 add.68
  91.2 0.1 add.69
  91.3 0.5 broadcast.100
  91.8 0.0 copy-done.1
  91.8 0.7 reduce.5
  92.5 0.1 reshape.111
  92.6 0.2 reduce_window_sum.24
  92.8 0.1 reduce_window_sum.25
  92.9 0.1 eq.38
  93.0 4.8 %scatter_custom_fusion.parent_ref = s32[128]{0:T(128)} fusion(s32[1024]{0:T(1024)S(1)} %bitcast.42, s32[1024]{0:T(1024)S(1)} %reshape.111, s32[]{:T(128)} %constant.12.clone.1), kind=kCustom, calls=%fused_computation.21 | custom fusion | bytes 516 | tf_op jit(solution)/shard_map/scatter | solution.py:71
  97.8 187.6 %all-to-all-done = f32[16,1024,128]{2,1,0:T(8,128)} async-done(((f32[16,1024,128]{2,1,0:T(8,128)}), f32[16,1024,128]{2,1,0:T(8,128)}, u32[]{:S(2)}, u32[]{:S(2)}) %all-to-all-start) | async-done | bytes 8388640 | tf_op jit(solution)/shard_map/all_to_all | solution.py:57
  285.4 7.4 %shard_map.75 = f32[128,2048]{1,0:T(8,128)} custom-call(s32[128]{0:T(128)} %scatter_custom_fusion.parent_ref, f32[128,128,128]{2,1,0:T(8,128)} %bitcast.12.incoming_ref, f32[128,2048]{1,0:T(8,128)} %bitcast.40), custom_call_target="tpu_custom_call" | custom-call | tf_op jit(solution)/shard_map/pallas_call | solution.py:149
  (7 shorter events, 0.1 us)
Async XLA Ops:
  7.4 2.3 copy-start
  7.4 54.6 %all-reduce.2.cloned.1.call-start = ((), (), s32[]{:S(2)}) async-start(), calls=%async_computation.1 | async-start | bytes 2097152 | tf_op jit(solution)/shard_map/psum | solution.py:16
  8.5 58.4 %all-gather.3.cloned.1.call-start = ((), (), s32[]{:S(2)}) async-start(), calls=%async_computation.2 | async-start | bytes 5242880 | tf_op jit(solution)/shard_map/all_gather | solution.py:22
  81.1 10.7 %copy-start.1 = (s32[16,1,1,64,1]{3,4,2,1,0:T(1,128)S(1)}, s32[16,1,1,64,1]{3,4,2,1,0:T(1,128)}, u32[]{:S(2)}) copy-start(s32[16,1,1,64,1]{3,4,2,1,0:T(1,128)} %param.13) | copy-start | bytes 12292
  81.2 204.3 %all-to-all-start = ((f32[16,1024,128]{2,1,0:T(8,128)}), f32[16,1024,128]{2,1,0:T(8,128)}, u32[]{:S(2)}, u32[]{:S(2)}) async-start(f32[16,1024,128]{2,1,0:T(8,128)} %bitcast.38), calls=%async_computation | async-start | bytes 16777216 | tf_op jit(solution)/shard_map/all_to_all | solution.py:57
Sparse Core Ops, SparseCore 0:
  10.9 48.9 all-reduce.1
Sparse Core Ops, SparseCore 1:
  10.9 53.0 all-gather.2

commit v8 on v6

--- a/solution.py
+++ b/solution.py
@@ -18,7 +18,7 @@
 
 def shards(diag_block, panel, trailing, parent_front, front_order, dest_group, parent_block):
     precise_mode = lax.Precision.HIGHEST
-    slab_rows = spread(panel[0], "row", 0)
+    slab_rows = lax.all_gather(panel[0], "row", axis=0, tiled=True)[: panel.shape[1]]
     col_rows = lax.all_gather(panel[0], "col", axis=0, tiled=True)
     chol_inv = factor_inverse(diag_block[0])
     contract_t = (((1,), (1,)), ((), ()))

time: 301 us -> 346 us (1.15)
  waiting for transfers between devices: 188 us -> 236 us
    all_gather x1, waiting for transfers between devices: 0.03 us -> 46.6 us  [shards(): col_rows = lax.all_gather(panel[0], 'col', axis=0, tiled=True)]
  transfers between devices with their start and end apart: 3 -> 3, of which waited for: 1 -> 2; matrix products, arithmetic and copies ran while one was open for 4% -> 4% of each run, Pallas kernels for 17% -> 15%
where the time goes in v8:
time: 346 us; the launch traced here: 345 us
  waiting for transfers between devices  236 us (68%)
  Pallas kernels  63.9 us (18%)
  between operations  14.1 us (4%)
  matrix products  12.7 us (4%)
  starting transfers between devices  9.3 us (3%)
  local copies, waits for them, and re-layouts  7.66 us (2%)
    all_to_all x1, waiting for transfers between devices, shards(): lax.all_to_all(outgoing.reshape(groups, capacity * BS, BS), 'cube', split...  188 us
    pallas_call x1, Pallas kernels, factor_inverse(): pl.pallas_call(factor_kernel, out_shape=jax.ShapeDtypeStruct((n, n), a.dt...  50.5 us
    all_gather x1, waiting for transfers between devices, shards(): col_rows = lax.all_gather(panel[0], 'col', axis=0, tiled=True)  46.6 us
    all_to_all x1, starting transfers between devices, shards(): lax.all_to_all(outgoing.reshape(groups, capacity * BS, BS), 'cube', split...  9.26 us
    dot_general x1, matrix products, shards(): lax.dot_general(slab_solved, col_rows, contract_t, precision=split_mode)  7.93 us
    pallas_call x1, Pallas kernels, combine_blocks(): pl.pallas_call(combine_kernel, out_shape=jax.ShapeDtypeStruct(front.shape...  6.96 us
  transfers between devices with their start and end apart: 3, of which 2 were waited for; matrix products, arithmetic and copies ran while one was open for 4% of the time, Pallas kernels for 15%

profile of v8, /device:TPU:87, one launch (start us, length us, event | category | flops | bytes accessed | tf_op | source)
XLA Modules:
  0.0 344.6 jit_solution(11539602971713910463)
XLA Ops:
  6.5 0.0 copy-start
  6.5 0.0 all-gather.5.cloned.1.call-start
  6.5 0.7 all-gather.5.cloned.1.call-update
  7.3 0.0 all-gather.7.cloned.1.call-start
  7.3 0.7 all-gather.7.cloned.1.call-update
  8.7 0.7 fusion.12
  9.3 0.1 fusion.6
  9.4 0.1 reduce_window_sum.26
  9.5 50.5 %shard_map.73 = f32[512,512]{1,0:T(8,128)} custom-call(f32[512,512]{1,0:T(8,128)} %bitcast.39), custom_call_target="tpu_custom_call" | custom-call | tf_op jit(solution)/shard_map/pallas_call | solution.py:210
  60.0 0.2 select_reduce_fusion
  60.2 0.0 copy-done
  60.2 1.3 scatter_custom_fusion.1.source_ref
  61.5 0.0 all-gather.5.cloned.1.call-done
  61.6 2.6 fusion.5
  64.1 2.2 fusion.13
  66.4 46.6 %all-gather.7.cloned.1.call-done = f32[1,2048,512]{2,1,0:T(8,128)} async-done(((f32[1,512,512]{2,1,0:T(8,128)}), f32[1,2048,512]{2,1,0:T(8,128)}) %all-gather.7.cloned.1.call-update) | async-done | bytes 4194320 | tf_op jit(solution)/shard_map/all_gather | solution.py:22
  113.0 7.9 %fusion.2.update_ref = f32[512,2048]{1,0:T(8,128)} fusion(f32[1,512,2048]{2,1,0:T(8,128)} %param.9, f32[512,512]{1,0:T(8,128)S(1)} %fusion.13, f32[1,2048,512]{2,1,0:T(8,128)} %all-gather.7.cloned.1.call-done, pred[2048]{0:T(1024)(128)(4,1)S(1)} %add_compare_fusion), kind=kOutput, calls=%fused_computation.5 | convolution fusion | flops 3223322624 | bytes 13633536 | tf_op jit(solution)/shard_map/dot_general | solution.py:28
  120.9 6.4 %shard_map.74 = f32[128,128,128]{2,1,0:T(8,128)} custom-call(s32[128]{0:T(128)} %scatter_custom_fusion.1.source_ref, f32[512,2048]{1,0:T(8,128)} %fusion.2.update_ref), custom_call_target="tpu_custom_call" | custom-call | tf_op jit(solution)/shard_map/pallas_call | solution.py:108
  127.3 0.0 copy-start.1
  127.3 9.3 %all-to-all-start = ((f32[16,1024,128]{2,1,0:T(8,128)}), f32[16,1024,128]{2,1,0:T(8,128)}, u32[]{:S(2)}, u32[]{:S(2)}) async-start(f32[16,1024,128]{2,1,0:T(8,128)} %bitcast.38), calls=%async_computation | async-start | bytes 16777216 | tf_op jit(solution)/shard_map/all_to_all | solution.py:57
  136.6 0.1 add.66
  136.6 0.1 add.67
  136.7 0.5 broadcast.94
  137.2 0.0 copy-done.1
  137.2 0.7 reduce.5
  137.9 0.1 reshape.111
  138.0 0.2 reduce_window_sum.24
  138.2 0.1 reduce_window_sum.25
  138.3 0.1 eq.35
  138.4 4.8 %scatter_custom_fusion.parent_ref = s32[128]{0:T(128)} fusion(s32[1024]{0:T(1024)S(1)} %bitcast.42, s32[1024]{0:T(1024)S(1)} %reshape.111, s32[]{:T(128)} %constant.12.clone.1), kind=kCustom, calls=%fused_computation.22 | custom fusion | bytes 516 | tf_op jit(solution)/shard_map/scatter | solution.py:71
  143.2 187.6 %all-to-all-done = f32[16,1024,128]{2,1,0:T(8,128)} async-done(((f32[16,1024,128]{2,1,0:T(8,128)}), f32[16,1024,128]{2,1,0:T(8,128)}, u32[]{:S(2)}, u32[]{:S(2)}) %all-to-all-start) | async-done | bytes 8388640 | tf_op jit(solution)/shard_map/all_to_all | solution.py:57
  330.8 7.0 %shard_map.75 = f32[128,2048]{1,0:T(8,128)} custom-call(s32[128]{0:T(128)} %scatter_custom_fusion.parent_ref, f32[128,128,128]{2,1,0:T(8,128)} %bitcast.12.incoming_ref, f32[128,2048]{1,0:T(8,128)} %bitcast.40), custom_call_target="tpu_custom_call" | custom-call | tf_op jit(solution)/shard_map/pallas_call | solution.py:137
  (6 shorter events, 0.1 us)
Async XLA Ops:
  6.5 53.7 %copy-start = (s32[16,1,1,64,1]{3,4,2,1,0:T(1,128)S(1)}, s32[16,1,1,64,1]{3,4,2,1,0:T(1,128)}, u32[]{:S(2)}) copy-start(s32[16,1,1,64,1]{3,4,2,1,0:T(1,128)} %param.12) | copy-start | bytes 12292
  6.5 55.0 %all-gather.5.cloned.1.call-start = ((), (), s32[]{:S(2)}) async-start(), calls=%async_computation.1 | async-start | bytes 5242880 | tf_op jit(solution)/shard_map/all_gather | solution.py:21
  7.3 105.7 %all-gather.7.cloned.1.call-start = ((), (), s32[]{:S(2)}) async-start(), calls=%async_computation.2 | async-start | bytes 5242880 | tf_op jit(solution)/shard_map/all_gather | solution.py:22
  127.3 9.9 %copy-start.1 = (s32[16,1,1,64,1]{3,4,2,1,0:T(1,128)S(1)}, s32[16,1,1,64,1]{3,4,2,1,0:T(1,128)}, u32[]{:S(2)}) copy-start(s32[16,1,1,64,1]{3,4,2,1,0:T(1,128)} %param.13) | copy-start | bytes 12292
  127.3 203.5 %all-to-all-start = ((f32[16,1024,128]{2,1,0:T(8,128)}), f32[16,1024,128]{2,1,0:T(8,128)}, u32[]{:S(2)}, u32[]{:S(2)}) async-start(f32[16,1024,128]{2,1,0:T(8,128)} %bitcast.38), calls=%async_computation | async-start | bytes 16777216 | tf_op jit(solution)/shard_map/all_to_all | solution.py:57
Sparse Core Ops, SparseCore 0:
  9.2 50.9 all-gather.4
  61.9 50.9 all-gather.6

commit v9 on v6

--- a/solution.py
+++ b/solution.py
@@ -12,8 +12,10 @@
 
 
 def spread(value, axis, root):
+    count = lax.axis_size(axis)
+    received = [lax.ppermute(value, axis, [(root, k)]) for k in range(count) if k != root]
     mine = lax.axis_index(axis) == root
-    return lax.psum(jnp.where(mine, value, jnp.zeros_like(value)), axis)
+    return jnp.where(mine, value, sum(received[1:], received[0]))
 
 
 def shards(diag_block, panel, trailing, parent_front, front_order, dest_group, parent_block):

time: 301 us -> 302 us (level)
  starting transfers between devices: 10 us -> 13.7 us
    ppermute x0 -> x3, starting transfers between devices: none -> 3.67 us  [spread(): lax.ppermute(value, axis, [(root, k)])]
  transfers between devices with their start and end apart: 3 -> 5, of which waited for: 1 -> 1; matrix products, arithmetic and copies ran while one was open for 4% -> 5% of each run, Pallas kernels for 17% -> 17%
where the time goes in v9:
time: 302 us
  waiting for transfers between devices  188 us (62%)
  Pallas kernels  63.9 us (21%)
  between operations  14.2 us (5%)
  starting transfers between devices  13.7 us (5%)
  matrix products  11.9 us (4%)
  local copies, waits for them, and re-layouts  7.66 us (3%)
    all_to_all x1, waiting for transfers between devices, shards(): lax.all_to_all(outgoing.reshape(groups, capacity * BS, BS), 'cube', split...  188 us
    pallas_call x1, Pallas kernels, factor_inverse(): pl.pallas_call(factor_kernel, out_shape=jax.ShapeDtypeStruct((n, n), a.dt...  50.5 us
    all_to_all x1, starting transfers between devices, shards(): lax.all_to_all(outgoing.reshape(groups, capacity * BS, BS), 'cube', split...  9.99 us
    dot_general x1, matrix products, shards(): lax.dot_general(slab_solved, col_rows, contract_t, precision=split_mode)  7.94 us
    pallas_call x1, Pallas kernels, combine_blocks(): pl.pallas_call(combine_kernel, out_shape=jax.ShapeDtypeStruct(front.shape...  6.97 us
    pallas_call x1, Pallas kernels, pack_blocks(): pl.pallas_call(functools.partial(pack_kernel, block_cols), out_shape=jax....  6.37 us
  transfers between devices with their start and end apart: 5, of which 1 were waited for; matrix products, arithmetic and copies ran while one was open for 5% of the time, Pallas kernels for 17%

profile of v9, /device:TPU:87, one launch (start us, length us, event | category | flops | bytes accessed | tf_op | source)
XLA Modules:
  0.0 301.6 jit_solution(8466512182219657633)
XLA Ops:
  6.5 0.7 all-gather.3.cloned.1.call-update
  7.3 1.3 collective-permute-start.2
  8.6 0.7 collective-permute-start.1
  9.3 1.6 collective-permute-start
  11.6 0.7 fusion.16
  12.2 0.1 fusion.10
  12.3 0.1 reduce_window_sum.26
  12.4 50.5 %shard_map.73 = f32[512,512]{1,0:T(8,128)} custom-call(f32[512,512]{1,0:T(8,128)} %bitcast.44), custom_call_target="tpu_custom_call" | custom-call | tf_op jit(solution)/shard_map/pallas_call | solution.py:212
  62.9 0.2 select_reduce_fusion
  63.1 0.8 fusion.11
  63.9 1.3 scatter_custom_fusion.1.source_ref
  65.2 0.0 collective-permute-done.2
  65.2 0.0 collective-permute-done
  65.2 2.9 fusion.5
  68.1 1.0 fusion.18
  69.2 0.0 all-gather.3.cloned.1.call-done
  69.2 7.9 %fusion.2.update_ref = f32[512,2048]{1,0:T(8,128)} fusion(f32[1,512,2048]{2,1,0:T(8,128)} %param.9, f32[512,512]{1,0:T(8,128)S(1)} %fusion.18, f32[1,2048,512]{2,1,0:T(8,128)} %all-gather.3.cloned.1.call-done, pred[2048]{0:T(1024)(128)(4,1)S(1)} %add_compare_fusion), kind=kOutput, calls=%fused_computation.5 | convolution fusion | flops 3223322624 | bytes 13633536 | tf_op jit(solution)/shard_map/dot_general | solution.py:30
  77.1 6.4 %shard_map.74 = f32[128,128,128]{2,1,0:T(8,128)} custom-call(s32[128]{0:T(128)} %scatter_custom_fusion.1.source_ref, f32[512,2048]{1,0:T(8,128)} %fusion.2.update_ref), custom_call_target="tpu_custom_call" | custom-call | tf_op jit(solution)/shard_map/pallas_call | solution.py:110
  83.5 0.0 copy-start.2
  83.5 0.0 copy-start.1
  83.5 10.0 %all-to-all-start = ((f32[16,1024,128]{2,1,0:T(8,128)}), f32[16,1024,128]{2,1,0:T(8,128)}, u32[]{:S(2)}, u32[]{:S(2)}) async-start(f32[16,1024,128]{2,1,0:T(8,128)} %bitcast.40), calls=%async_computation | async-start | bytes 16777216 | tf_op jit(solution)/shard_map/all_to_all | solution.py:59
  93.5 0.1 add.72
  93.6 0.1 add.73
  93.7 0.5 broadcast.94
  94.2 0.7 reduce.5
  94.9 0.1 reshape.111
  95.0 0.2 reduce_window_sum.24
  95.2 0.1 reduce_window_sum.25
  95.3 0.1 eq.38
  95.4 4.8 %scatter_custom_fusion.parent_ref = s32[128]{0:T(128)} fusion(s32[1024]{0:T(1024)S(1)} %bitcast.47, s32[1024]{0:T(1024)S(1)} %reshape.111, s32[]{:T(128)} %constant.12.clone.1), kind=kCustom, calls=%fused_computation.25 | custom fusion | bytes 516 | tf_op jit(solution)/shard_map/scatter | solution.py:73
  100.2 187.6 %all-to-all-done = f32[16,1024,128]{2,1,0:T(8,128)} async-done(((f32[16,1024,128]{2,1,0:T(8,128)}), f32[16,1024,128]{2,1,0:T(8,128)}, u32[]{:S(2)}, u32[]{:S(2)}) %all-to-all-start) | async-done | bytes 8388640 | tf_op jit(solution)/shard_map/all_to_all | solution.py:59
  287.8 7.0 %shard_map.75 = f32[128,2048]{1,0:T(8,128)} custom-call(s32[128]{0:T(128)} %scatter_custom_fusion.parent_ref, f32[128,128,128]{2,1,0:T(8,128)} %bitcast.12.incoming_ref, f32[128,2048]{1,0:T(8,128)} %bitcast.45), custom_call_target="tpu_custom_call" | custom-call | tf_op jit(solution)/shard_map/pallas_call | solution.py:139
  (11 shorter events, 0.1 us)
Async XLA Ops:
  6.5 62.6 %all-gather.3.cloned.1.call-start = ((), (), s32[]{:S(2)}) async-start(), calls=%async_computation.1 | async-start | bytes 5242880 | tf_op jit(solution)/shard_map/all_gather | solution.py:24
  7.3 57.9 %collective-permute-start.2 = (f32[512,512]{1,0:T(8,128)}, f32[512,512]{1,0:T(8,128)S(1)}, u32[]{:S(2)}, u32[]{:S(2)}) collective-permute-start(f32[512,512]{1,0:T(8,128)} %bitcast.41), channel_id=1, source_target_pairs={{0,12},{1,13},{2,14},{3,15},{16,28},{17,29},{18,30},{19,31},{32,44... | collective-permute-start | bytes 3145736 | tf_op jit(solution)/shard_map/ppermute | solution.py:16
  8.6 56.6 %collective-permute-start.1 = (f32[512,512]{1,0:T(8,128)}, f32[512,512]{1,0:T(8,128)S(1)}, u32[]{:S(2)}, u32[]{:S(2)}) collective-permute-start(f32[512,512]{1,0:T(8,128)} %bitcast.42), channel_id=1, source_target_pairs={{0,8},{1,9},{2,10},{3,11},{16,24},{17,25},{18,26},{19,27},{32,40},... | collective-permute-start | bytes 3145736 | tf_op jit(solution)/shard_map/ppermute | solution.py:16
  9.3 55.9 %collective-permute-start = (f32[512,512]{1,0:T(8,128)}, f32[512,512]{1,0:T(8,128)}, u32[]{:S(2)}, u32[]{:S(2)}) collective-permute-start(f32[512,512]{1,0:T(8,128)} %bitcast.43), channel_id=1, source_target_pairs={{0,4},{1,5},{2,6},{3,7},{16,20},{17,21},{18,22},{19,23},{32,36},{3... | collective-permute-start | bytes 3145736 | tf_op jit(solution)/shard_map/ppermute | solution.py:16
  62.9 5.2 %copy-start = (f32[512,512]{1,0:T(8,128)S(1)}, f32[512,512]{1,0:T(8,128)}, u32[]{:S(2)}) copy-start(f32[512,512]{1,0:T(8,128)} %shard_map.73) | copy-start | bytes 3145732
  83.5 10.7 %copy-start.2 = (s32[16,1,1,64,1]{3,4,2,1,0:T(1,128)S(1)}, s32[16,1,1,64,1]{3,4,2,1,0:T(1,128)}, u32[]{:S(2)}) copy-start(s32[16,1,1,64,1]{3,4,2,1,0:T(1,128)} %param.13) | copy-start | bytes 12292
  83.5 11.4 %copy-start.1 = (s32[16,1,1,64,1]{3,4,2,1,0:T(1,128)S(1)}, s32[16,1,1,64,1]{3,4,2,1,0:T(1,128)}, u32[]{:S(2)}) copy-start(s32[16,1,1,64,1]{3,4,2,1,0:T(1,128)} %param.12) | copy-start | bytes 12292
  83.5 204.3 %all-to-all-start = ((f32[16,1024,128]{2,1,0:T(8,128)}), f32[16,1024,128]{2,1,0:T(8,128)}, u32[]{:S(2)}, u32[]{:S(2)}) async-start(f32[16,1024,128]{2,1,0:T(8,128)} %bitcast.40), calls=%async_computation | async-start | bytes 16777216 | tf_op jit(solution)/shard_map/all_to_all | solution.py:59
Sparse Core Ops, SparseCore 0:
  9.2 51.9 all-gather.2

commit v10 on v6

--- a/solution.py
+++ b/solution.py
@@ -99,8 +99,8 @@
 
         return carry
 
-    lax.fori_loop(0, nslots, start, 0)
-    lax.fori_loop(0, nslots, finish, 0)
+    lax.fori_loop(0, nslots, start, 0, unroll=8)
+    lax.fori_loop(0, nslots, finish, 0, unroll=8)
 
 
 def pack_blocks(source_of_slot, update, block_cols):
@@ -130,7 +130,7 @@
 
         return carry
 
-    lax.fori_loop(0, incoming_ref.shape[0], body, 0)
+    lax.fori_loop(0, incoming_ref.shape[0], body, 0, unroll=8)
 
 
 def combine_blocks(parent_of_slot, incoming, front):

time: 301 us -> 299 us (level)
  no operation moved by 1% of the time
where the time goes in v10:
time: 299 us; the launch traced here: 298 us
  waiting for transfers between devices  188 us (63%)
  Pallas kernels  62.4 us (21%)
  between operations  15.6 us (5%)
  matrix products  12.7 us (4%)
  starting transfers between devices  10 us (3%)
  local copies, waits for them, and re-layouts  7 us (2%)
    all_to_all x1, waiting for transfers between devices, shards(): lax.all_to_all(outgoing.reshape(groups, capacity * BS, BS), 'cube', split...  188 us
    pallas_call x1, Pallas kernels, factor_inverse(): pl.pallas_call(factor_kernel, out_shape=jax.ShapeDtypeStruct((n, n), a.dt...  50.6 us
    all_to_all x1, starting transfers between devices, shards(): lax.all_to_all(outgoing.reshape(groups, capacity * BS, BS), 'cube', split...  9.96 us
    dot_general x1, matrix products, shards(): lax.dot_general(slab_solved, col_rows, contract_t, precision=split_mode)  7.94 us
    pallas_call x1, Pallas kernels, combine_blocks(): pl.pallas_call(combine_kernel, out_shape=jax.ShapeDtypeStruct(front.shape...  6.53 us
  transfers between devices with their start and end apart: 3, of which 1 were waited for; matrix products, arithmetic and copies ran while one was open for 4% of the time, Pallas kernels for 17%

profile of v10, /device:TPU:87, one launch (start us, length us, event | category | flops | bytes accessed | tf_op | source)
XLA Modules:
  0.0 298.3 jit_solution(4000020403081808448)
XLA Ops:
  7.4 0.0 copy-start
  7.4 0.0 all-reduce.2.cloned.1.call-start
  7.4 1.1 select_bitcast_fusion
  8.4 0.0 all-reduce.2.cloned.1.call-update
  8.5 0.0 all-gather.3.cloned.1.call-start
  8.5 0.5 all-gather.3.cloned.1.call-update
  9.7 0.0 copy-done
  9.7 0.1 fusion.5
  9.8 0.1 reduce_window_sum.26
  9.9 50.6 %shard_map.73 = f32[512,512]{1,0:T(8,128)} custom-call(f32[512,512]{1,0:T(8,128)} %bitcast.39), custom_call_target="tpu_custom_call" | custom-call | tf_op jit(solution)/shard_map/pallas_call | solution.py:210
  60.5 0.2 select_reduce_fusion
  60.7 1.3 scatter_custom_fusion.1.source_ref
  62.0 0.0 all-reduce.2.cloned.1.call-done
  62.0 2.6 fusion.12
  64.6 2.2 fusion.13
  66.8 0.0 all-gather.3.cloned.1.call-done
  66.8 7.9 %fusion.2.update_ref = f32[512,2048]{1,0:T(8,128)} fusion(f32[1,512,2048]{2,1,0:T(8,128)} %param.9, f32[512,512]{1,0:T(8,128)S(1)} %fusion.13, f32[1,2048,512]{2,1,0:T(8,128)} %all-gather.3.cloned.1.call-done, pred[2048]{0:T(1024)(128)(4,1)S(1)} %add_compare_fusion), kind=kOutput, calls=%fused_computation.5 | convolution fusion | flops 3223322624 | bytes 13633536 | tf_op jit(solution)/shard_map/dot_general | solution.py:28
  74.8 5.3 %shard_map.74 = f32[128,128,128]{2,1,0:T(8,128)} custom-call(s32[128]{0:T(128)} %scatter_custom_fusion.1.source_ref, f32[512,2048]{1,0:T(8,128)} %fusion.2.update_ref), custom_call_target="tpu_custom_call" | custom-call | tf_op jit(solution)/shard_map/pallas_call | solution.py:108
  80.1 0.0 copy-start.1
  80.1 10.0 %all-to-all-start = ((f32[16,1024,128]{2,1,0:T(8,128)}), f32[16,1024,128]{2,1,0:T(8,128)}, u32[]{:S(2)}, u32[]{:S(2)}) async-start(f32[16,1024,128]{2,1,0:T(8,128)} %bitcast.38), calls=%async_computation | async-start | bytes 16777216 | tf_op jit(solution)/shard_map/all_to_all | solution.py:57
  90.1 0.1 add.68
  90.2 0.1 add.69
  90.2 0.5 broadcast.100
  90.7 0.0 copy-done.1
  90.7 0.7 reduce.5
  91.4 0.1 reshape.111
  91.5 0.2 reduce_window_sum.24
  91.8 0.1 reduce_window_sum.25
  91.8 0.1 eq.38
  91.9 4.8 %scatter_custom_fusion.parent_ref = s32[128]{0:T(128)} fusion(s32[1024]{0:T(1024)S(1)} %bitcast.42, s32[1024]{0:T(1024)S(1)} %reshape.111, s32[]{:T(128)} %constant.12.clone.1), kind=kCustom, calls=%fused_computation.21 | custom fusion | bytes 516 | tf_op jit(solution)/shard_map/scatter | solution.py:71
  96.7 187.6 %all-to-all-done = f32[16,1024,128]{2,1,0:T(8,128)} async-done(((f32[16,1024,128]{2,1,0:T(8,128)}), f32[16,1024,128]{2,1,0:T(8,128)}, u32[]{:S(2)}, u32[]{:S(2)}) %all-to-all-start) | async-done | bytes 8388640 | tf_op jit(solution)/shard_map/all_to_all | solution.py:57
  284.4 6.5 %shard_map.75 = f32[128,2048]{1,0:T(8,128)} custom-call(s32[128]{0:T(128)} %scatter_custom_fusion.parent_ref, f32[128,128,128]{2,1,0:T(8,128)} %bitcast.12.incoming_ref, f32[128,2048]{1,0:T(8,128)} %bitcast.40), custom_call_target="tpu_custom_call" | custom-call | tf_op jit(solution)/shard_map/pallas_call | solution.py:137
  (7 shorter events, 0.1 us)
Async XLA Ops:
  7.4 2.3 copy-start
  7.4 54.6 %all-reduce.2.cloned.1.call-start = ((), (), s32[]{:S(2)}) async-start(), calls=%async_computation.1 | async-start | bytes 2097152 | tf_op jit(solution)/shard_map/psum | solution.py:16
  8.5 58.4 %all-gather.3.cloned.1.call-start = ((), (), s32[]{:S(2)}) async-start(), calls=%async_computation.2 | async-start | bytes 5242880 | tf_op jit(solution)/shard_map/all_gather | solution.py:22
  80.1 10.6 %copy-start.1 = (s32[16,1,1,64,1]{3,4,2,1,0:T(1,128)S(1)}, s32[16,1,1,64,1]{3,4,2,1,0:T(1,128)}, u32[]{:S(2)}) copy-start(s32[16,1,1,64,1]{3,4,2,1,0:T(1,128)} %param.13) | copy-start | bytes 12292
  80.1 204.2 %all-to-all-start = ((f32[16,1024,128]{2,1,0:T(8,128)}), f32[16,1024,128]{2,1,0:T(8,128)}, u32[]{:S(2)}, u32[]{:S(2)}) async-start(f32[16,1024,128]{2,1,0:T(8,128)} %bitcast.38), calls=%async_computation | async-start | bytes 16777216 | tf_op jit(solution)/shard_map/all_to_all | solution.py:57
Sparse Core Ops, SparseCore 0:
  10.9 48.9 all-reduce.1
Sparse Core Ops, SparseCore 1:
  10.9 53.0 all-gather.2

commit v11 on v10

--- a/solution.py
+++ b/solution.py
@@ -99,8 +99,8 @@
 
         return carry
 
-    lax.fori_loop(0, nslots, start, 0, unroll=8)
-    lax.fori_loop(0, nslots, finish, 0, unroll=8)
+    lax.fori_loop(0, nslots, start, 0, unroll=True)
+    lax.fori_loop(0, nslots, finish, 0, unroll=True)
 
 
 def pack_blocks(source_of_slot, update, block_cols):
@@ -130,7 +130,7 @@
 
         return carry
 
-    lax.fori_loop(0, incoming_ref.shape[0], body, 0, unroll=8)
+    lax.fori_loop(0, incoming_ref.shape[0], body, 0, unroll=True)
 
 
 def combine_blocks(parent_of_slot, incoming, front):

time: 299 us -> 299 us (level)
  no operation moved by 1% of the time
where the time goes in v11:
time: 299 us; the launch traced here: 298 us
  waiting for transfers between devices  188 us (63%)
  Pallas kernels  62 us (21%)
  between operations  15.6 us (5%)
  matrix products  12.7 us (4%)
  starting transfers between devices  10 us (3%)
  local copies, waits for them, and re-layouts  7 us (2%)
    all_to_all x1, waiting for transfers between devices, shards(): lax.all_to_all(outgoing.reshape(groups, capacity * BS, BS), 'cube', split...  188 us
    pallas_call x1, Pallas kernels, factor_inverse(): pl.pallas_call(factor_kernel, out_shape=jax.ShapeDtypeStruct((n, n), a.dt...  50.6 us
    all_to_all x1, starting transfers between devices, shards(): lax.all_to_all(outgoing.reshape(groups, capacity * BS, BS), 'cube', split...  9.98 us
    dot_general x1, matrix products, shards(): lax.dot_general(slab_solved, col_rows, contract_t, precision=split_mode)  7.94 us
    pallas_call x1, Pallas kernels, combine_blocks(): pl.pallas_call(combine_kernel, out_shape=jax.ShapeDtypeStruct(front.shape...  6.15 us
  transfers between devices with their start and end apart: 3, of which 1 were waited for; matrix products, arithmetic and copies ran while one was open for 4% of the time, Pallas kernels for 17%

profile of v11, /device:TPU:87, one launch (start us, length us, event | category | flops | bytes accessed | tf_op | source)
XLA Modules:
  0.0 297.9 jit_solution(2233452075324925676)
XLA Ops:
  7.4 0.0 copy-start
  7.4 0.0 all-reduce.2.cloned.1.call-start
  7.4 1.1 select_bitcast_fusion
  8.4 0.0 all-reduce.2.cloned.1.call-update
  8.5 0.0 all-gather.3.cloned.1.call-start
  8.5 0.5 all-gather.3.cloned.1.call-update
  9.7 0.0 copy-done
  9.7 0.1 fusion.5
  9.8 0.1 reduce_window_sum.26
  9.9 50.6 %shard_map.73 = f32[512,512]{1,0:T(8,128)} custom-call(f32[512,512]{1,0:T(8,128)} %bitcast.39), custom_call_target="tpu_custom_call" | custom-call | tf_op jit(solution)/shard_map/pallas_call | solution.py:210
  60.5 0.2 select_reduce_fusion
  60.7 1.3 scatter_custom_fusion.1.source_ref
  62.0 0.0 all-reduce.2.cloned.1.call-done
  62.0 2.6 fusion.12
  64.6 2.2 fusion.13
  66.8 0.0 all-gather.3.cloned.1.call-done
  66.8 7.9 %fusion.2.update_ref = f32[512,2048]{1,0:T(8,128)} fusion(f32[1,512,2048]{2,1,0:T(8,128)} %param.9, f32[512,512]{1,0:T(8,128)S(1)} %fusion.13, f32[1,2048,512]{2,1,0:T(8,128)} %all-gather.3.cloned.1.call-done, pred[2048]{0:T(1024)(128)(4,1)S(1)} %add_compare_fusion), kind=kOutput, calls=%fused_computation.5 | convolution fusion | flops 3223322624 | bytes 13633536 | tf_op jit(solution)/shard_map/dot_general | solution.py:28
  74.8 5.3 %shard_map.74 = f32[128,128,128]{2,1,0:T(8,128)} custom-call(s32[128]{0:T(128)} %scatter_custom_fusion.1.source_ref, f32[512,2048]{1,0:T(8,128)} %fusion.2.update_ref), custom_call_target="tpu_custom_call" | custom-call | tf_op jit(solution)/shard_map/pallas_call | solution.py:108
  80.1 0.0 copy-start.1
  80.1 10.0 %all-to-all-start = ((f32[16,1024,128]{2,1,0:T(8,128)}), f32[16,1024,128]{2,1,0:T(8,128)}, u32[]{:S(2)}, u32[]{:S(2)}) async-start(f32[16,1024,128]{2,1,0:T(8,128)} %bitcast.38), calls=%async_computation | async-start | bytes 16777216 | tf_op jit(solution)/shard_map/all_to_all | solution.py:57
  90.1 0.1 add.68
  90.1 0.1 add.69
  90.2 0.5 broadcast.100
  90.7 0.0 copy-done.1
  90.7 0.7 reduce.5
  91.4 0.1 reshape.111
  91.5 0.2 reduce_window_sum.24
  91.7 0.1 reduce_window_sum.25
  91.8 0.1 eq.38
  91.9 4.8 %scatter_custom_fusion.parent_ref = s32[128]{0:T(128)} fusion(s32[1024]{0:T(1024)S(1)} %bitcast.42, s32[1024]{0:T(1024)S(1)} %reshape.111, s32[]{:T(128)} %constant.12.clone.1), kind=kCustom, calls=%fused_computation.21 | custom fusion | bytes 516 | tf_op jit(solution)/shard_map/scatter | solution.py:71
  96.7 187.6 %all-to-all-done = f32[16,1024,128]{2,1,0:T(8,128)} async-done(((f32[16,1024,128]{2,1,0:T(8,128)}), f32[16,1024,128]{2,1,0:T(8,128)}, u32[]{:S(2)}, u32[]{:S(2)}) %all-to-all-start) | async-done | bytes 8388640 | tf_op jit(solution)/shard_map/all_to_all | solution.py:57
  284.3 6.1 %shard_map.75 = f32[128,2048]{1,0:T(8,128)} custom-call(s32[128]{0:T(128)} %scatter_custom_fusion.parent_ref, f32[128,128,128]{2,1,0:T(8,128)} %bitcast.12.incoming_ref, f32[128,2048]{1,0:T(8,128)} %bitcast.40), custom_call_target="tpu_custom_call" | custom-call | tf_op jit(solution)/shard_map/pallas_call | solution.py:137
  (7 shorter events, 0.1 us)
Async XLA Ops:
  7.4 2.3 copy-start
  7.4 54.6 %all-reduce.2.cloned.1.call-start = ((), (), s32[]{:S(2)}) async-start(), calls=%async_computation.1 | async-start | bytes 2097152 | tf_op jit(solution)/shard_map/psum | solution.py:16
  8.5 58.4 %all-gather.3.cloned.1.call-start = ((), (), s32[]{:S(2)}) async-start(), calls=%async_computation.2 | async-start | bytes 5242880 | tf_op jit(solution)/shard_map/all_gather | solution.py:22
  80.1 10.7 %copy-start.1 = (s32[16,1,1,64,1]{3,4,2,1,0:T(1,128)S(1)}, s32[16,1,1,64,1]{3,4,2,1,0:T(1,128)}, u32[]{:S(2)}) copy-start(s32[16,1,1,64,1]{3,4,2,1,0:T(1,128)} %param.13) | copy-start | bytes 12292
  80.1 204.3 %all-to-all-start = ((f32[16,1024,128]{2,1,0:T(8,128)}), f32[16,1024,128]{2,1,0:T(8,128)}, u32[]{:S(2)}, u32[]{:S(2)}) async-start(f32[16,1024,128]{2,1,0:T(8,128)} %bitcast.38), calls=%async_computation | async-start | bytes 16777216 | tf_op jit(solution)/shard_map/all_to_all | solution.py:57
Sparse Core Ops, SparseCore 0:
  10.9 48.9 all-reduce.1
Sparse Core Ops, SparseCore 1:
  10.9 53.0 all-gather.2

commit v12 on v10

--- a/solution.py
+++ b/solution.py
@@ -122,12 +122,9 @@
 
     def body(slot, carry):
         parent = parent_ref[slot]
-
-        @pl.when(parent >= 0)
-        def _():
-            cols = pl.ds(pl.multiple_of(parent * BS, BS), BS)
-            out_ref[:, cols] = out_ref[:, cols] + incoming_ref[slot]
-
+        cols = pl.ds(pl.multiple_of(jnp.maximum(parent, 0) * BS, BS), BS)
+        addend = jnp.where(parent >= 0, incoming_ref[slot], jnp.float32(0.0))
+        out_ref[:, cols] = out_ref[:, cols] + addend
         return carry
 
     lax.fori_loop(0, incoming_ref.shape[0], body, 0, unroll=8)

time: 299 us -> 299 us (level)
  no operation moved by 1% of the time
where the time goes in v12:
time: 299 us; the launch traced here: 298 us
  waiting for transfers between devices  188 us (63%)
  Pallas kernels  62.6 us (21%)
  between operations  15.6 us (5%)
  matrix products  12.7 us (4%)
  starting transfers between devices  9.98 us (3%)
  local copies, waits for them, and re-layouts  7 us (2%)
    all_to_all x1, waiting for transfers between devices, shards(): lax.all_to_all(outgoing.reshape(groups, capacity * BS, BS), 'cube', split...  188 us
    pallas_call x1, Pallas kernels, factor_inverse(): pl.pallas_call(factor_kernel, out_shape=jax.ShapeDtypeStruct((n, n), a.dt...  50.6 us
    all_to_all x1, starting transfers between devices, shards(): lax.all_to_all(outgoing.reshape(groups, capacity * BS, BS), 'cube', split...  9.93 us
    dot_general x1, matrix products, shards(): lax.dot_general(slab_solved, col_rows, contract_t, precision=split_mode)  7.94 us
    pallas_call x1, Pallas kernels, combine_blocks(): pl.pallas_call(combine_kernel, out_shape=jax.ShapeDtypeStruct(front.shape...  6.64 us
  transfers between devices with their start and end apart: 3, of which 1 were waited for; matrix products, arithmetic and copies ran while one was open for 4% of the time, Pallas kernels for 17%

profile of v12, /device:TPU:87, one launch (start us, length us, event | category | flops | bytes accessed | tf_op | source)
XLA Modules:
  0.0 298.4 jit_solution(17924837179681928726)
XLA Ops:
  7.4 0.0 copy-start
  7.4 0.0 all-reduce.2.cloned.1.call-start
  7.4 1.1 select_bitcast_fusion
  8.4 0.0 all-reduce.2.cloned.1.call-update
  8.5 0.0 all-gather.3.cloned.1.call-start
  8.5 0.5 all-gather.3.cloned.1.call-update
  9.7 0.0 copy-done
  9.7 0.1 fusion.5
  9.8 0.1 reduce_window_sum.26
  9.9 50.6 %shard_map.73 = f32[512,512]{1,0:T(8,128)} custom-call(f32[512,512]{1,0:T(8,128)} %bitcast.39), custom_call_target="tpu_custom_call" | custom-call | tf_op jit(solution)/shard_map/pallas_call | solution.py:207
  60.5 0.2 select_reduce_fusion
  60.7 1.3 scatter_custom_fusion.1.source_ref
  62.0 0.0 all-reduce.2.cloned.1.call-done
  62.0 2.6 fusion.12
  64.6 2.2 fusion.13
  66.8 0.0 all-gather.3.cloned.1.call-done
  66.8 7.9 %fusion.2.update_ref = f32[512,2048]{1,0:T(8,128)} fusion(f32[1,512,2048]{2,1,0:T(8,128)} %param.9, f32[512,512]{1,0:T(8,128)S(1)} %fusion.13, f32[1,2048,512]{2,1,0:T(8,128)} %all-gather.3.cloned.1.call-done, pred[2048]{0:T(1024)(128)(4,1)S(1)} %add_compare_fusion), kind=kOutput, calls=%fused_computation.5 | convolution fusion | flops 3223322624 | bytes 13633536 | tf_op jit(solution)/shard_map/dot_general | solution.py:28
  74.8 5.4 %shard_map.74 = f32[128,128,128]{2,1,0:T(8,128)} custom-call(s32[128]{0:T(128)} %scatter_custom_fusion.1.source_ref, f32[512,2048]{1,0:T(8,128)} %fusion.2.update_ref), custom_call_target="tpu_custom_call" | custom-call | tf_op jit(solution)/shard_map/pallas_call | solution.py:108
  80.1 0.0 copy-start.1
  80.1 9.9 %all-to-all-start = ((f32[16,1024,128]{2,1,0:T(8,128)}), f32[16,1024,128]{2,1,0:T(8,128)}, u32[]{:S(2)}, u32[]{:S(2)}) async-start(f32[16,1024,128]{2,1,0:T(8,128)} %bitcast.38), calls=%async_computation | async-start | bytes 16777216 | tf_op jit(solution)/shard_map/all_to_all | solution.py:57
  90.1 0.1 add.68
  90.1 0.1 add.69
  90.2 0.5 broadcast.100
  90.7 0.0 copy-done.1
  90.7 0.7 reduce.5
  91.4 0.1 reshape.111
  91.5 0.2 reduce_window_sum.24
  91.7 0.1 reduce_window_sum.25
  91.8 0.1 eq.38
  91.9 4.8 %scatter_custom_fusion.parent_ref = s32[128]{0:T(128)} fusion(s32[1024]{0:T(1024)S(1)} %bitcast.42, s32[1024]{0:T(1024)S(1)} %reshape.111, s32[]{:T(128)} %constant.12.clone.1), kind=kCustom, calls=%fused_computation.21 | custom fusion | bytes 516 | tf_op jit(solution)/shard_map/scatter | solution.py:71
  96.7 187.6 %all-to-all-done = f32[16,1024,128]{2,1,0:T(8,128)} async-done(((f32[16,1024,128]{2,1,0:T(8,128)}), f32[16,1024,128]{2,1,0:T(8,128)}, u32[]{:S(2)}, u32[]{:S(2)}) %all-to-all-start) | async-done | bytes 8388640 | tf_op jit(solution)/shard_map/all_to_all | solution.py:57
  284.3 6.6 %shard_map.75 = f32[128,2048]{1,0:T(8,128)} custom-call(s32[128]{0:T(128)} %scatter_custom_fusion.parent_ref, f32[128,128,128]{2,1,0:T(8,128)} %bitcast.12.incoming_ref, f32[128,2048]{1,0:T(8,128)} %bitcast.40), custom_call_target="tpu_custom_call" | custom-call | tf_op jit(solution)/shard_map/pallas_call | solution.py:134
  (7 shorter events, 0.1 us)
Async XLA Ops:
  7.4 2.3 copy-start
  7.4 54.6 %all-reduce.2.cloned.1.call-start = ((), (), s32[]{:S(2)}) async-start(), calls=%async_computation.1 | async-start | bytes 2097152 | tf_op jit(solution)/shard_map/psum | solution.py:16
  8.5 58.4 %all-gather.3.cloned.1.call-start = ((), (), s32[]{:S(2)}) async-start(), calls=%async_computation.2 | async-start | bytes 5242880 | tf_op jit(solution)/shard_map/all_gather | solution.py:22
  80.1 10.6 %copy-start.1 = (s32[16,1,1,64,1]{3,4,2,1,0:T(1,128)S(1)}, s32[16,1,1,64,1]{3,4,2,1,0:T(1,128)}, u32[]{:S(2)}) copy-start(s32[16,1,1,64,1]{3,4,2,1,0:T(1,128)} %param.13) | copy-start | bytes 12292
  80.1 204.2 %all-to-all-start = ((f32[16,1024,128]{2,1,0:T(8,128)}), f32[16,1024,128]{2,1,0:T(8,128)}, u32[]{:S(2)}, u32[]{:S(2)}) async-start(f32[16,1024,128]{2,1,0:T(8,128)} %bitcast.38), calls=%async_computation | async-start | bytes 16777216 | tf_op jit(solution)/shard_map/all_to_all | solution.py:57
Sparse Core Ops, SparseCore 0:
  10.9 48.9 all-reduce.1
Sparse Core Ops, SparseCore 1:
  10.9 53.0 all-gather.2

commit v13 on v10

--- a/solution.py
+++ b/solution.py
@@ -198,9 +198,9 @@
     for i in range(1, nb):
         ii = pl.ds(i * BS, BS)
         left = pl.ds(0, i * BS)
-        mixed = jnp.dot(work_ref[ii, left], inv_ref[left, left], precision=hp,
+        mixed = jnp.dot(work_ref[ii, left], inv_ref[left, left], precision=lax.Precision.HIGH,
                         preferred_element_type=jnp.float32)
-        inv_ref[ii, left] = -jnp.dot(diag_inv[i], mixed, precision=hp,
+        inv_ref[ii, left] = -jnp.dot(diag_inv[i], mixed, precision=lax.Precision.HIGH,
                                      preferred_element_type=jnp.float32)
         inv_ref[ii, ii] = diag_inv[i]
 

time: 299 us -> 299 us (level)
  no operation moved by 1% of the time
where the time goes in v13:
time: 299 us; the launch traced here: 298 us
  waiting for transfers between devices  188 us (63%)
  Pallas kernels  62.4 us (21%)
  between operations  15.6 us (5%)
  matrix products  12.7 us (4%)
  starting transfers between devices  10 us (3%)
  local copies, waits for them, and re-layouts  7 us (2%)
    all_to_all x1, waiting for transfers between devices, shards(): lax.all_to_all(outgoing.reshape(groups, capacity * BS, BS), 'cube', split...  188 us
    pallas_call x1, Pallas kernels, factor_inverse(): pl.pallas_call(factor_kernel, out_shape=jax.ShapeDtypeStruct((n, n), a.dt...  50.5 us
    all_to_all x1, starting transfers between devices, shards(): lax.all_to_all(outgoing.reshape(groups, capacity * BS, BS), 'cube', split...  9.98 us
    dot_general x1, matrix products, shards(): lax.dot_general(slab_solved, col_rows, contract_t, precision=split_mode)  7.94 us
    pallas_call x1, Pallas kernels, combine_blocks(): pl.pallas_call(combine_kernel, out_shape=jax.ShapeDtypeStruct(front.shape...  6.52 us
  transfers between devices with their start and end apart: 3, of which 1 were waited for; matrix products, arithmetic and copies ran while one was open for 4% of the time, Pallas kernels for 17%

profile of v13, /device:TPU:87, one launch (start us, length us, event | category | flops | bytes accessed | tf_op | source)
XLA Modules:
  0.0 298.3 jit_solution(4027000800147281784)
XLA Ops:
  7.4 0.0 copy-start
  7.4 0.0 all-reduce.2.cloned.1.call-start
  7.4 1.1 select_bitcast_fusion
  8.4 0.0 all-reduce.2.cloned.1.call-update
  8.5 0.0 all-gather.3.cloned.1.call-start
  8.5 0.5 all-gather.3.cloned.1.call-update
  9.7 0.0 copy-done
  9.7 0.1 fusion.5
  9.8 0.1 reduce_window_sum.26
  9.9 50.5 %shard_map.73 = f32[512,512]{1,0:T(8,128)} custom-call(f32[512,512]{1,0:T(8,128)} %bitcast.39), custom_call_target="tpu_custom_call" | custom-call | tf_op jit(solution)/shard_map/pallas_call | solution.py:210
  60.3 0.2 select_reduce_fusion
  60.6 1.3 scatter_custom_fusion.1.source_ref
  61.9 0.0 all-reduce.2.cloned.1.call-done
  61.9 2.6 fusion.12
  64.4 2.2 fusion.13
  66.7 0.0 all-gather.3.cloned.1.call-done
  66.7 7.9 %fusion.2.update_ref = f32[512,2048]{1,0:T(8,128)} fusion(f32[1,512,2048]{2,1,0:T(8,128)} %param.9, f32[512,512]{1,0:T(8,128)S(1)} %fusion.13, f32[1,2048,512]{2,1,0:T(8,128)} %all-gather.3.cloned.1.call-done, pred[2048]{0:T(1024)(128)(4,1)S(1)} %add_compare_fusion), kind=kOutput, calls=%fused_computation.5 | convolution fusion | flops 3223322624 | bytes 13633536 | tf_op jit(solution)/shard_map/dot_general | solution.py:28
  74.7 5.4 %shard_map.74 = f32[128,128,128]{2,1,0:T(8,128)} custom-call(s32[128]{0:T(128)} %scatter_custom_fusion.1.source_ref, f32[512,2048]{1,0:T(8,128)} %fusion.2.update_ref), custom_call_target="tpu_custom_call" | custom-call | tf_op jit(solution)/shard_map/pallas_call | solution.py:108
  80.1 0.0 copy-start.1
  80.1 10.0 %all-to-all-start = ((f32[16,1024,128]{2,1,0:T(8,128)}), f32[16,1024,128]{2,1,0:T(8,128)}, u32[]{:S(2)}, u32[]{:S(2)}) async-start(f32[16,1024,128]{2,1,0:T(8,128)} %bitcast.38), calls=%async_computation | async-start | bytes 16777216 | tf_op jit(solution)/shard_map/all_to_all | solution.py:57
  90.1 0.1 add.68
  90.1 0.1 add.69
  90.2 0.5 broadcast.100
  90.7 0.0 copy-done.1
  90.7 0.7 reduce.5
  91.4 0.1 reshape.111
  91.5 0.2 reduce_window_sum.24
  91.7 0.1 reduce_window_sum.25
  91.8 0.1 eq.38
  91.9 4.8 %scatter_custom_fusion.parent_ref = s32[128]{0:T(128)} fusion(s32[1024]{0:T(1024)S(1)} %bitcast.42, s32[1024]{0:T(1024)S(1)} %reshape.111, s32[]{:T(128)} %constant.12.clone.1), kind=kCustom, calls=%fused_computation.21 | custom fusion | bytes 516 | tf_op jit(solution)/shard_map/scatter | solution.py:71
  96.7 187.6 %all-to-all-done = f32[16,1024,128]{2,1,0:T(8,128)} async-done(((f32[16,1024,128]{2,1,0:T(8,128)}), f32[16,1024,128]{2,1,0:T(8,128)}, u32[]{:S(2)}, u32[]{:S(2)}) %all-to-all-start) | async-done | bytes 8388640 | tf_op jit(solution)/shard_map/all_to_all | solution.py:57
  284.4 6.5 %shard_map.75 = f32[128,2048]{1,0:T(8,128)} custom-call(s32[128]{0:T(128)} %scatter_custom_fusion.parent_ref, f32[128,128,128]{2,1,0:T(8,128)} %bitcast.12.incoming_ref, f32[128,2048]{1,0:T(8,128)} %bitcast.40), custom_call_target="tpu_custom_call" | custom-call | tf_op jit(solution)/shard_map/pallas_call | solution.py:137
  (7 shorter events, 0.1 us)
Async XLA Ops:
  7.4 2.3 copy-start
  7.4 54.5 %all-reduce.2.cloned.1.call-start = ((), (), s32[]{:S(2)}) async-start(), calls=%async_computation.1 | async-start | bytes 2097152 | tf_op jit(solution)/shard_map/psum | solution.py:16
  8.5 58.2 %all-gather.3.cloned.1.call-start = ((), (), s32[]{:S(2)}) async-start(), calls=%async_computation.2 | async-start | bytes 5242880 | tf_op jit(solution)/shard_map/all_gather | solution.py:22
  80.1 10.7 %copy-start.1 = (s32[16,1,1,64,1]{3,4,2,1,0:T(1,128)S(1)}, s32[16,1,1,64,1]{3,4,2,1,0:T(1,128)}, u32[]{:S(2)}) copy-start(s32[16,1,1,64,1]{3,4,2,1,0:T(1,128)} %param.13) | copy-start | bytes 12292
  80.1 204.3 %all-to-all-start = ((f32[16,1024,128]{2,1,0:T(8,128)}), f32[16,1024,128]{2,1,0:T(8,128)}, u32[]{:S(2)}, u32[]{:S(2)}) async-start(f32[16,1024,128]{2,1,0:T(8,128)} %bitcast.38), calls=%async_computation | async-start | bytes 16777216 | tf_op jit(solution)/shard_map/all_to_all | solution.py:57
Sparse Core Ops, SparseCore 0:
  10.9 49.0 all-reduce.1
Sparse Core Ops, SparseCore 1:
  10.9 53.0 all-gather.2

commit v14 on v10

--- a/solution.py
+++ b/solution.py
@@ -146,12 +146,14 @@
     )(parent_of_slot, incoming, front)
 
 
-def factor_kernel(a_ref, inv_ref, work_ref, g_ref):
+def factor_kernel(a_ref, inv_ref, work_ref, g_ref, load_sem):
     n = a_ref.shape[0]
     nb = n // BS
     hp = lax.Precision.HIGHEST
     nt = (((1,), (1,)), ((), ()))
-    work_ref[...] = a_ref[...]
+    load = pltpu.make_async_copy(a_ref, work_ref, load_sem)
+    load.start()
+    load.wait()
     lane = lax.broadcasted_iota(jnp.int32, (1, 2 * BS), 1)
     sub = lax.broadcasted_iota(jnp.int32, (BS, BS), 0)
     col = lax.broadcasted_iota(jnp.int32, (BS, BS), 1)
@@ -210,9 +212,13 @@
     return pl.pallas_call(
         factor_kernel,
         out_shape=jax.ShapeDtypeStruct((n, n), a.dtype),
-        in_specs=[pl.BlockSpec(memory_space=pltpu.VMEM)],
+        in_specs=[pl.BlockSpec(memory_space=pl.ANY)],
         out_specs=pl.BlockSpec(memory_space=pltpu.VMEM),
-        scratch_shapes=[pltpu.VMEM((n, n), jnp.float32), pltpu.VMEM((BS, 2 * BS), jnp.float32)],
+        scratch_shapes=[
+            pltpu.VMEM((n, n), jnp.float32),
+            pltpu.VMEM((BS, 2 * BS), jnp.float32),
+            pltpu.SemaphoreType.DMA(()),
+        ],
     )(a)
 
 def solution(mesh):

time: 299 us -> 299 us (level)
  no operation moved by 1% of the time
where the time goes in v14:
time: 299 us; the launch traced here: 298 us
  waiting for transfers between devices  188 us (63%)
  Pallas kernels  62.3 us (21%)
  between operations  15.6 us (5%)
  matrix products  12.7 us (4%)
  starting transfers between devices  9.97 us (3%)
  local copies, waits for them, and re-layouts  7 us (2%)
    all_to_all x1, waiting for transfers between devices, shards(): lax.all_to_all(outgoing.reshape(groups, capacity * BS, BS), 'cube', split...  188 us
    pallas_call x1, Pallas kernels, factor_inverse(): pl.pallas_call(factor_kernel, out_shape=jax.ShapeDtypeStruct((n, n), a.dt...  50.6 us
    all_to_all x1, starting transfers between devices, shards(): lax.all_to_all(outgoing.reshape(groups, capacity * BS, BS), 'cube', split...  9.92 us
    dot_general x1, matrix products, shards(): lax.dot_general(slab_solved, col_rows, contract_t, precision=split_mode)  7.94 us
    pallas_call x1, Pallas kernels, combine_blocks(): pl.pallas_call(combine_kernel, out_shape=jax.ShapeDtypeStruct(front.shape...  6.36 us
  transfers between devices with their start and end apart: 3, of which 1 were waited for; matrix products, arithmetic and copies ran while one was open for 4% of the time, Pallas kernels for 17%

profile of v14, /device:TPU:87, one launch (start us, length us, event | category | flops | bytes accessed | tf_op | source)
XLA Modules:
  0.0 298.2 jit_solution(8891311273413567537)
XLA Ops:
  7.4 0.0 copy-start
  7.4 0.0 all-reduce.2.cloned.1.call-start
  7.4 1.1 select_bitcast_fusion
  8.4 0.0 all-reduce.2.cloned.1.call-update
  8.5 0.0 all-gather.3.cloned.1.call-start
  8.5 0.5 all-gather.3.cloned.1.call-update
  9.7 0.0 copy-done
  9.7 0.1 fusion.5
  9.8 0.1 reduce_window_sum.26
  9.9 50.6 %shard_map.73 = f32[512,512]{1,0:T(8,128)} custom-call(f32[512,512]{1,0:T(8,128)} %bitcast.39), custom_call_target="tpu_custom_call" | custom-call | tf_op jit(solution)/shard_map/pallas_call | solution.py:212
  60.5 0.2 select_reduce_fusion
  60.7 1.3 scatter_custom_fusion.1.source_ref
  62.0 0.0 all-reduce.2.cloned.1.call-done
  62.0 2.6 fusion.12
  64.6 2.2 fusion.13
  66.8 0.0 all-gather.3.cloned.1.call-done
  66.9 7.9 %fusion.2.update_ref = f32[512,2048]{1,0:T(8,128)} fusion(f32[1,512,2048]{2,1,0:T(8,128)} %param.9, f32[512,512]{1,0:T(8,128)S(1)} %fusion.13, f32[1,2048,512]{2,1,0:T(8,128)} %all-gather.3.cloned.1.call-done, pred[2048]{0:T(1024)(128)(4,1)S(1)} %add_compare_fusion), kind=kOutput, calls=%fused_computation.5 | convolution fusion | flops 3223322624 | bytes 13633536 | tf_op jit(solution)/shard_map/dot_general | solution.py:28
  74.8 5.4 %shard_map.74 = f32[128,128,128]{2,1,0:T(8,128)} custom-call(s32[128]{0:T(128)} %scatter_custom_fusion.1.source_ref, f32[512,2048]{1,0:T(8,128)} %fusion.2.update_ref), custom_call_target="tpu_custom_call" | custom-call | tf_op jit(solution)/shard_map/pallas_call | solution.py:108
  80.2 0.0 copy-start.1
  80.2 9.9 %all-to-all-start = ((f32[16,1024,128]{2,1,0:T(8,128)}), f32[16,1024,128]{2,1,0:T(8,128)}, u32[]{:S(2)}, u32[]{:S(2)}) async-start(f32[16,1024,128]{2,1,0:T(8,128)} %bitcast.38), calls=%async_computation | async-start | bytes 16777216 | tf_op jit(solution)/shard_map/all_to_all | solution.py:57
  90.1 0.1 add.68
  90.2 0.1 add.69
  90.3 0.5 broadcast.100
  90.8 0.0 copy-done.1
  90.8 0.7 reduce.5
  91.5 0.1 reshape.111
  91.6 0.2 reduce_window_sum.24
  91.8 0.1 reduce_window_sum.25
  91.9 0.1 eq.38
  92.0 4.8 %scatter_custom_fusion.parent_ref = s32[128]{0:T(128)} fusion(s32[1024]{0:T(1024)S(1)} %bitcast.42, s32[1024]{0:T(1024)S(1)} %reshape.111, s32[]{:T(128)} %constant.12.clone.1), kind=kCustom, calls=%fused_computation.21 | custom fusion | bytes 516 | tf_op jit(solution)/shard_map/scatter | solution.py:71
  96.8 187.6 %all-to-all-done = f32[16,1024,128]{2,1,0:T(8,128)} async-done(((f32[16,1024,128]{2,1,0:T(8,128)}), f32[16,1024,128]{2,1,0:T(8,128)}, u32[]{:S(2)}, u32[]{:S(2)}) %all-to-all-start) | async-done | bytes 8388640 | tf_op jit(solution)/shard_map/all_to_all | solution.py:57
  284.4 6.4 %shard_map.75 = f32[128,2048]{1,0:T(8,128)} custom-call(s32[128]{0:T(128)} %scatter_custom_fusion.parent_ref, f32[128,128,128]{2,1,0:T(8,128)} %bitcast.12.incoming_ref, f32[128,2048]{1,0:T(8,128)} %bitcast.40), custom_call_target="tpu_custom_call" | custom-call | tf_op jit(solution)/shard_map/pallas_call | solution.py:137
  (7 shorter events, 0.1 us)
Async XLA Ops:
  7.4 2.3 copy-start
  7.4 54.6 %all-reduce.2.cloned.1.call-start = ((), (), s32[]{:S(2)}) async-start(), calls=%async_computation.1 | async-start | bytes 2097152 | tf_op jit(solution)/shard_map/psum | solution.py:16
  8.5 58.4 %all-gather.3.cloned.1.call-start = ((), (), s32[]{:S(2)}) async-start(), calls=%async_computation.2 | async-start | bytes 5242880 | tf_op jit(solution)/shard_map/all_gather | solution.py:22
  80.2 10.6 %copy-start.1 = (s32[16,1,1,64,1]{3,4,2,1,0:T(1,128)S(1)}, s32[16,1,1,64,1]{3,4,2,1,0:T(1,128)}, u32[]{:S(2)}) copy-start(s32[16,1,1,64,1]{3,4,2,1,0:T(1,128)} %param.13) | copy-start | bytes 12292
  80.2 204.2 %all-to-all-start = ((f32[16,1024,128]{2,1,0:T(8,128)}), f32[16,1024,128]{2,1,0:T(8,128)}, u32[]{:S(2)}, u32[]{:S(2)}) async-start(f32[16,1024,128]{2,1,0:T(8,128)} %bitcast.38), calls=%async_computation | async-start | bytes 16777216 | tf_op jit(solution)/shard_map/all_to_all | solution.py:57
Sparse Core Ops, SparseCore 0:
  10.9 48.9 all-reduce.1
Sparse Core Ops, SparseCore 1:
  10.9 53.0 all-gather.2
